TPU v7x, 32 devices: a whole 2x2x4 slice. The times are simulated.
32 devices in a mesh: lat: 4 (over x, core), lon: 8 (over z, y).
Axes of the slice: x: 2, y: 2, z: 4, core: 2. Of those that a mesh axis runs over, the one named last changes fastest.
Arguments:
- tokens: bfloat16 [64, 128, 1024], P('lat', 'lon'), may hold values from -6 to 6
- norm_gain: float32 [1024], replicated, may hold values from 0.25 to 1.75
- w_qkv: bfloat16 [1024, 3072], replicated, may hold values from -0.1875 to 0.1875
- w_out: bfloat16 [1024, 1024], replicated, may hold values from -0.1875 to 0.1875
- cotangent: bfloat16 [64, 128, 1024], P('lat', 'lon'), may hold values from -6 to 6
Outputs:
- result: bfloat16 [64, 128, 1024], P('lat', 'lon')
- grad_tokens: bfloat16 [64, 128, 1024], P('lat', 'lon')
- grad_w_qkv: float32 [1024, 3072], P(('lat', 'lon'))
- grad_w_out: float32 [1024, 1024], P(('lat', 'lon'))
All inputs are finite; a program needn't handle non-finite values.
Results may differ from a plain program's by a relative error of at most 0.025.
Values may be sent and summed in bfloat16 or wider, within the bound.
A program may use at most 192 MiB of HBM per device.

v0:
```python
import jax
import jax.numpy as jnp
from jax import lax
from jax.sharding import PartitionSpec as P

H = 16
R = 6


epsilon = 1e-06
floor_score = -1e30


def with_halo(cells, sides, width):
    for axis, dim in sides:
        count = lax.axis_size(axis)
        head = lax.slice_in_dim(cells, 0, width, axis=dim)
        tail = lax.slice_in_dim(cells, cells.shape[dim] - width, cells.shape[dim], axis=dim)
        cells = jnp.concatenate(
            [
                lax.ppermute(tail, axis, [(i, (i + 1) % count) for i in range(count)]),
                cells,
                lax.ppermute(head, axis, [((i + 1) % count, i) for i in range(count)]),
            ],
            axis=dim,
        )
    return cells


def shifted(value, axis, steps):
    count = lax.axis_size(axis)
    pairs = [(source, (source + steps) % count) for source in range(count)]
    return lax.ppermute(value, axis, pairs)


def to_tiles(grid, side):
    rows_all, cols_all, depth = grid.shape
    shaped = grid.reshape(rows_all // side, side, cols_all // side, side, depth)
    return shaped.transpose(0, 2, 1, 3, 4).reshape(-1, side * side, depth)


def from_tiles(tiled, rows_all, cols_all, side):
    depth = tiled.shape[-1]
    shaped = tiled.reshape(rows_all // side, cols_all // side, side, side, depth)
    return shaped.transpose(0, 2, 1, 3, 4).reshape(rows_all, cols_all, depth)


def region_places(tile_rows, tile_cols, side, extent):
    row_place = (jnp.arange(tile_rows) * side)[:, None, None, None] + jnp.arange(extent)[
        None, None, :, None
    ]
    col_place = (jnp.arange(tile_cols) * side)[None, :, None, None] + jnp.arange(extent)[
        None, None, None, :
    ]
    return (row_place, col_place)


def to_regions(framed, tile_rows, tile_cols, side):
    depth = framed.shape[-1]
    extent = side + framed.shape[0] - tile_rows * side
    row_place, col_place = region_places(tile_rows, tile_cols, side, extent)
    picked = framed[row_place, col_place]
    return picked.reshape(tile_rows * tile_cols, extent * extent, depth)


def from_regions(parts, tile_rows, tile_cols, side, keep_rows, keep_cols):
    depth = parts.shape[-1]
    extent = side + keep_rows - tile_rows * side
    row_place, col_place = region_places(tile_rows, tile_cols, side, extent)
    pieces = parts.reshape(tile_rows, tile_cols, extent, extent, depth)
    summed = jnp.zeros((keep_rows, keep_cols, depth), jnp.float32)
    return summed.at[row_place, col_place].add(pieces)


def window_mask(side, radius):
    extent = side + 2 * radius
    query_at = jnp.arange(side * side)
    key_at = jnp.arange(extent * extent)
    row_gap = key_at[None, :] // extent - query_at[:, None] // side
    col_gap = key_at[None, :] % extent - query_at[:, None] % side
    return (row_gap >= 0) & (row_gap <= 2 * radius) & (col_gap >= 0) & (col_gap <= 2 * radius)


def pole_pack(north_rows, south_rows):
    return jnp.stack([north_rows, south_rows])


def pole_split(arrived):
    return (arrived[0], arrived[1])


def fill_poles(framed, arrived, radius, at_north, at_south):
    north_in, south_in = pole_split(arrived)
    length = framed.shape[0]
    top_rows = jnp.where(at_north, north_in, framed[:radius])
    bottom_rows = jnp.where(at_south, south_in, framed[length - radius :])
    return jnp.concatenate([top_rows, framed[radius : length - radius], bottom_rows], axis=0)


def shards(tokens, norm_gain, w_qkv, w_out, cotangent):
    lat_rows, lon_cols, model_width = tokens.shape
    head_count = H
    head_size = model_width // head_count
    radius = R
    side = 8
    tile_rows = lat_rows // side
    tile_cols = lon_cols // side
    tile_total = tile_rows * tile_cols
    tile_cells = side * side
    region_size = (side + 2 * radius) * (side + 2 * radius)
    scale_qk = head_size ** (-0.5)
    lat_count = lax.axis_size("lat")
    lon_count = lax.axis_size("lon")
    half_circle = lon_count // 2
    lat_place = lax.axis_index("lat")
    at_north = lat_place == 0
    at_south = lat_place == lat_count - 1
    device_count = lat_count * lon_count
    grad_scale = (lat_rows * lon_cols * device_count) ** (-0.5)
    allowed = window_mask(side, radius)
    source = tokens.astype(jnp.float32)
    inverse = lax.rsqrt(jnp.mean(source * source, axis=-1, keepdims=True) + epsilon)
    normed = (source * inverse * norm_gain).astype(jnp.bfloat16)
    flat_normed = normed.reshape(-1, model_width)
    packed = jnp.dot(flat_normed, w_qkv, preferred_element_type=jnp.float32).astype(jnp.bfloat16)
    query_grid = packed[:, :model_width].reshape(lat_rows, lon_cols, model_width)
    keyval_grid = packed[:, model_width:].reshape(lat_rows, lon_cols, 2 * model_width)
    framed = with_halo(keyval_grid, (("lat", 0), ("lon", 1)), radius)
    north_rows = framed[radius : 2 * radius][::-1]
    south_rows = framed[lat_rows : lat_rows + radius][::-1]
    arrived = shifted(pole_pack(north_rows, south_rows), "lon", half_circle)
    framed = fill_poles(framed, arrived, radius, at_north, at_south)
    keyval_regions = to_regions(framed, tile_rows, tile_cols, side)
    key_regions = keyval_regions[..., :model_width].reshape(
        tile_total, region_size, head_count, head_size
    )
    value_regions = keyval_regions[..., model_width:].reshape(
        tile_total, region_size, head_count, head_size
    )
    query_tiles = to_tiles(query_grid, side).reshape(tile_total, tile_cells, head_count, head_size)
    scores = (
        jnp.einsum("tqhd,tkhd->thqk", query_tiles, key_regions, preferred_element_type=jnp.float32)
        * scale_qk
    )
    masked = jnp.where(allowed, scores, floor_score)
    highest = jnp.max(masked, axis=-1, keepdims=True)
    log_total = highest + jnp.log(jnp.sum(jnp.exp(masked - highest), axis=-1, keepdims=True))
    chances = jnp.exp(masked - log_total)
    chances_low = chances.astype(jnp.bfloat16)
    attended_tiles = jnp.einsum(
        "thqk,tkhd->tqhd", chances_low, value_regions, preferred_element_type=jnp.float32
    ).astype(jnp.bfloat16)
    attended_grid = from_tiles(
        attended_tiles.reshape(tile_total, tile_cells, model_width), lat_rows, lon_cols, side
    )
    attended_flat = attended_grid.reshape(-1, model_width)
    source_flat = source.reshape(-1, model_width)
    mixed = jnp.dot(attended_flat, w_out, preferred_element_type=jnp.float32) + source_flat
    result = mixed.astype(jnp.bfloat16).reshape(lat_rows, lon_cols, model_width)
    grad_flat = cotangent.reshape(-1, model_width)
    grad_attended = jnp.dot(grad_flat, w_out.T, preferred_element_type=jnp.float32).astype(
        jnp.bfloat16
    )
    grad_att_grid = grad_attended.reshape(lat_rows, lon_cols, model_width)
    product = grad_attended.astype(jnp.float32) * attended_flat.astype(jnp.float32)
    delta_grid = product.reshape(lat_rows, lon_cols, head_count, head_size).sum(axis=-1)
    delta_tiles = to_tiles(delta_grid, side).transpose(0, 2, 1)[..., None]
    grad_tiles = to_tiles(grad_att_grid, side).reshape(
        tile_total, tile_cells, head_count, head_size
    )
    grad_chances = jnp.einsum(
        "tqhd,tkhd->thqk", grad_tiles, value_regions, preferred_element_type=jnp.float32
    )
    grad_scores = (chances * (grad_chances - delta_tiles)).astype(jnp.bfloat16)
    grad_query_tiles = (
        jnp.einsum("thqk,tkhd->tqhd", grad_scores, key_regions, preferred_element_type=jnp.float32)
        * scale_qk
    )
    grad_query = from_tiles(
        grad_query_tiles.reshape(tile_total, tile_cells, model_width), lat_rows, lon_cols, side
    )
    grad_key_regions = (
        jnp.einsum("thqk,tqhd->tkhd", grad_scores, query_tiles, preferred_element_type=jnp.float32)
        * scale_qk
    )
    grad_value_regions = jnp.einsum(
        "thqk,tqhd->tkhd", chances_low, grad_tiles, preferred_element_type=jnp.float32
    )
    partial_regions = jnp.concatenate(
        [
            grad_key_regions.reshape(tile_total, region_size, model_width),
            grad_value_regions.reshape(tile_total, region_size, model_width),
        ],
        axis=-1,
    )
    spread = from_regions(
        partial_regions, tile_rows, tile_cols, side, lat_rows + 2 * radius, lon_cols + 2 * radius
    )
    north_back = spread[:radius][::-1]
    south_back = spread[lat_rows + radius :][::-1]
    returned = shifted(
        pole_pack(north_back, south_back).astype(jnp.bfloat16), "lon", half_circle
    ).astype(jnp.float32)
    north_in, south_in = pole_split(returned)
    spread = spread.at[:radius].set(
        jnp.where(at_north, jnp.zeros_like(north_back), spread[:radius])
    )
    spread = spread.at[lat_rows + radius :].set(
        jnp.where(at_south, jnp.zeros_like(south_back), spread[lat_rows + radius :])
    )
    spread = spread.at[radius : 2 * radius].add(jnp.where(at_north, north_in, 0.0))
    spread = spread.at[lat_rows : lat_rows + radius].add(jnp.where(at_south, south_in, 0.0))
    gathered = with_halo(spread.astype(jnp.bfloat16), (("lat", 0), ("lon", 1)), radius).astype(
        spread.dtype
    )
    folded = gathered[2 * radius : 2 * radius + lat_rows]
    folded = folded.at[:radius].add(gathered[:radius])
    folded = folded.at[lat_rows - radius :].add(gathered[lat_rows + 3 * radius :])
    grad_keyval = folded[:, 2 * radius : 2 * radius + lon_cols]
    grad_keyval = grad_keyval.at[:, :radius].add(folded[:, :radius])
    grad_keyval = grad_keyval.at[:, lon_cols - radius :].add(folded[:, lon_cols + 3 * radius :])
    grad_packed = (
        jnp.concatenate([grad_query, grad_keyval], axis=-1)
        .reshape(-1, 3 * model_width)
        .astype(jnp.bfloat16)
    )
    grad_normed = jnp.dot(grad_packed, w_qkv.T, preferred_element_type=jnp.float32)
    scaled = norm_gain * grad_normed
    inverse_flat = inverse.reshape(-1, 1)
    grad_input = (
        grad_flat.astype(jnp.float32)
        + inverse_flat * scaled
        - source_flat * inverse_flat**3 * jnp.mean(source_flat * scaled, axis=-1, keepdims=True)
    )
    grad_tokens = grad_input.astype(jnp.bfloat16).reshape(lat_rows, lon_cols, model_width)
    qkv_term = jnp.dot(flat_normed.T, grad_packed, preferred_element_type=jnp.float32)
    out_whole = jnp.dot(attended_flat.T, grad_flat, preferred_element_type=jnp.float32)
    qkv_share, out_share = (
        lax.psum_scatter(qkv_term, ("lat", "lon"), scatter_dimension=0, tiled=True),
        lax.psum_scatter(out_whole, ("lat", "lon"), scatter_dimension=0, tiled=True),
    )
    return (result, grad_tokens, qkv_share * grad_scale, out_share * grad_scale)


def solution(mesh):
    placed = (P("lat", "lon", None), P(), P(), P(), P("lat", "lon", None))
    return jax.shard_map(
        shards,
        mesh=mesh,
        in_specs=placed,
        out_specs=(
            P("lat", "lon", None),
            P("lat", "lon", None),
            P(("lat", "lon"), None),
            P(("lat", "lon"), None),
        ),
        check_vma=False,
    )
```

profile of v0, /device:TPU:0, one launch (start us, length us, event | category | flops | bytes accessed | tf_op | source)
XLA Modules:
  0.0 779.8 jit_solution(5749525775959901289)
XLA Ops:
  9.9 4.8 convolution_convert_fusion
  14.7 2.4 collective-permute-start.1
  17.2 9.4 %collective-permute-done.1 = bf16[6,16,2048]{2,1,0:T(8,128)(2,1)S(1)} collective-permute-done((bf16[6,16,2048]{2,1,0:T(8,128)(2,1)S(1)}, bf16[6,16,2048]{2,1,0:T(8,128)(2,1)S(1)}, u32[]{:S(2)}, u32[]{:S(2)}) %collective-permute-start.1) | collective-permute-done | bytes 393248 | tf_op jit(solution)/shard_map/ppermute | solution.py:23
  28.7 4.6 collective-permute-start.3
  34.0 30.3 %collective-permute-done.3 = bf16[28,6,2048]{2,0,1:T(8,128)(2,1)S(1)} collective-permute-done((bf16[28,6,2048]{2,0,1:T(8,128)(2,1)S(1)}, bf16[28,6,2048]{2,0,1:T(8,128)(2,1)S(1)}, u32[]{:S(2)}, u32[]{:S(2)}) %collective-permute-start.3) | collective-permute-done | bytes 688160 | tf_op jit(solution)/shard_map/ppermute | solution.py:23
  65.1 2.0 pad_maximum_fusion.1
  69.4 2.5 copy.36
  71.9 2.6 collective-permute-start.4
  77.2 2.0 copy.51
  79.4 54.9 %collective-permute-done.4 = bf16[2,6,28,2048]{3,0,2,1:T(2,128)(2,1)} collective-permute-done((bf16[2,6,28,2048]{3,0,2,1:T(2,128)(2,1)}, bf16[2,6,28,2048]{3,0,2,1:T(2,128)(2,1)}, u32[]{:S(2)}, u32[]{:S(2)}) %collective-permute-start.4) | collective-permute-done | bytes 1376288 | tf_op jit(solution)/shard_map/ppermute | solution.py:33
  134.2 4.4 fusion.46
  140.3 2.3 pad_maximum_fusion.2
  142.5 42.9 %gather_fusion = bf16[1600,2048]{1,0:T(8,128)(2,1)} fusion(bf16[28,28,2048]{2,1,0:T(8,128)(2,1)} %pad_maximum_fusion.2, s32[1600]{0:T(1024)S(1)} %reshape.504), kind=kCustom, calls=%fused_computation | custom fusion | bytes 13120000 | tf_op jit(solution)/shard_map/gather | solution.py:62
  185.4 6.4 fusion.41
  191.8 6.1 copy.65
  197.9 6.1 copy.64
  203.9 4.1 fusion.1
  208.0 2.3 exponential_reduce_fusion
  210.3 2.0 copy-done.1
  213.2 3.4 fusion.13
  216.6 2.7 copy.43
  219.4 1.9 reshape_reshape.24
  225.6 2.4 copy.53
  228.0 2.8 reshape.494
  230.9 2.2 reduce_sum.38
  233.2 9.3 %convolution_bitcast_fusion = f32[4,400,16,64]{1,3,2,0:T(8,128)} fusion(bf16[4,64,16,64]{1,3,2,0:T(8,128)(2,1)S(1)} %copy.53, f32[4,16,64,400]{3,2,1,0:T(8,128)} %copy-done.1, f32[4,16,64]{2,1,0:T(8,128)S(1)} %log_add_fusion, pred[64,400]{1,0:T(8,128)(4,1)S(1)} %fusion.25), kind=kOutput, calls=%fused_computation.16 | convolution fusion | flops 216268800 | bytes 13673472 | tf_op jit(solution)/shard_map/thqk,tqhd->tkhd/dot_general | solution.py:186
  242.5 5.6 multiply_convert_fusion
  248.1 2.0 copy-done.4
  250.1 4.6 multiply_bitcast_fusion
  254.6 11.5 %copy.52 = f32[4,400,16,64]{3,2,0,1:T(8,128)} copy(f32[4,400,16,64]{1,3,2,0:T(8,128)} %multiply_bitcast_fusion) | data formatting | bytes 13107200 | tf_op jit(solution)/shard_map/mul | solution.py:183
  266.2 12.4 %concatenate.57 = f32[2,2,20,20,1024]{4,1,0,3,2:T(2,128)} reshape(f32[4,400,16,64]{3,2,0,1:T(8,128)} %copy.52) | data formatting | bytes 13107200 | tf_op jit(solution)/shard_map/concatenate | solution.py:189
  278.6 11.5 %copy.54 = f32[4,400,16,64]{3,2,0,1:T(8,128)} copy(f32[4,400,16,64]{1,3,2,0:T(8,128)} %convolution_bitcast_fusion) | data formatting | bytes 13107200 | tf_op jit(solution)/shard_map/thqk,tqhd->tkhd/transpose | solution.py:186
  290.1 12.4 %concatenate.58 = f32[2,2,20,20,1024]{4,1,0,3,2:T(2,128)} reshape(f32[4,400,16,64]{3,2,0,1:T(8,128)} %copy.54) | data formatting | bytes 13107200 | tf_op jit(solution)/shard_map/concatenate | solution.py:189
  302.5 13.1 %pad_maximum_fusion = f32[2,2,20,20,2048]{4,1,0,3,2:T(2,128)} fusion(f32[2,2,20,20,1024]{4,1,0,3,2:T(2,128)} %concatenate.58, f32[2,2,20,20,1024]{4,1,0,3,2:T(2,128)} %concatenate.57), kind=kLoop, calls=%fused_computation.2 | loop fusion | flops 3276800 | bytes 26214400 | tf_op jit(solution)/shard_map/concatenate | solution.py:189
  315.7 17.8 %copy.55 = f32[2,2,20,20,2048]{4,3,2,1,0:T(8,128)} copy(f32[2,2,20,20,2048]{4,1,0,3,2:T(2,128)} %pad_maximum_fusion) | data formatting | bytes 26214400 | tf_op jit(solution)/shard_map/concatenate | solution.py:189
  333.5 15.4 %reshape.512 = f32[1600,2048]{1,0:T(8,128)} reshape(f32[2,2,20,20,2048]{4,3,2,1,0:T(8,128)} %copy.55) | data formatting | bytes 26214400 | tf_op jit(solution)/shard_map/concatenate | solution.py:189
  348.9 30.5 %scatter_custom_fusion = f32[784,2048]{1,0:T(8,128)} fusion(s32[1600]{0:T(1024)S(1)} %reshape.510, f32[1600,2048]{1,0:T(8,128)} %reshape.512, f32[]{:T(128)} %constant.279.clone.1), kind=kCustom, calls=%fused_computation.14 | custom fusion | flops 3276800 | bytes 6423040
  379.3 2.4 slice.349
  381.8 2.1 reshape.503
  383.9 2.1 fusion.22
  390.2 2.5 copy.56
  392.7 2.7 fusion.47
  395.5 7.3 reshape.501
  404.2 2.7 fusion.12
  406.9 66.0 %collective-permute-done.5 = bf16[2,6,28,2048]{3,0,2,1:T(2,128)(2,1)} collective-permute-done((bf16[2,6,28,2048]{3,0,2,1:T(2,128)(2,1)}, bf16[2,6,28,2048]{3,0,2,1:T(2,128)(2,1)}, u32[]{:S(2)}, u32[]{:S(2)}) %collective-permute-start.5) | collective-permute-done | bytes 1376288 | tf_op jit(solution)/shard_map/ppermute | solution.py:33
  472.9 1.9 copy_convert_fusion
  474.8 2.8 fusion.11
  477.7 2.9 fusion.8
  480.5 3.7 convert_element_type.63
  486.2 14.5 %collective-permute-done.6 = bf16[6,28,2048]{2,1,0:T(8,128)(2,1)S(1)} collective-permute-done((bf16[6,28,2048]{2,1,0:T(8,128)(2,1)S(1)}, bf16[6,28,2048]{2,1,0:T(8,128)(2,1)S(1)}, u32[]{:S(2)}, u32[]{:S(2)}) %collective-permute-start.6) | collective-permute-done | bytes 688160 | tf_op jit(solution)/shard_map/ppermute | solution.py:21
  500.7 2.5 collective-permute-done.7
  506.3 5.4 collective-permute-start.9
  514.9 2.2 fusion.14
  517.1 2.7 copy.49
  519.8 2.6 reshape_reshape.28
  522.4 2.0 copy.50
  524.4 54.6 %collective-permute-done.9 = bf16[40,6,2048]{2,0,1:T(8,128)(2,1)} collective-permute-done((bf16[40,6,2048]{2,0,1:T(8,128)(2,1)}, bf16[40,6,2048]{2,0,1:T(8,128)(2,1)}, u32[]{:S(2)}, u32[]{:S(2)}) %collective-permute-start.9) | collective-permute-done | bytes 983072 | tf_op jit(solution)/shard_map/ppermute | solution.py:23
  582.6 3.4 maximum_convert_fusion
  592.4 6.2 scatter-add.42
  598.5 2.9 slice_add_fusion
  601.4 5.4 scatter-add.43
  609.6 7.4 fusion.20
  619.6 5.3 fusion.19
  627.6 143.2 %reduce-scatter.3.cloned.1.call-done = f32[32,3072]{1,0:T(8,128)} async-done(((f32[1024,3072]{1,0:T(8,128)}), f32[32,3072]{1,0:T(8,128)}) %reduce-scatter.3.cloned.1.call-update) | async-done | bytes 393232 | tf_op jit(solution)/shard_map/reduce_scatter | solution.py:239
  (139 shorter events, 51.6 us)
Async XLA Ops:
  7.2 215.0 %copy-start = (bf16[1024,1024]{1,0:T(8,128)(2,1)S(1)}, bf16[1024,1024]{1,0:T(8,128)(2,1)}, u32[]{:S(2)}) copy-start(bf16[1024,1024]{1,0:T(8,128)(2,1)} %param.24) | copy-start | bytes 6291460
  7.2 618.8 %reduce-scatter.5.cloned.1.call-start = ((), (), s32[]{:S(2)}) async-start(), calls=%async_computation.3 | async-start | bytes 4325376 | tf_op jit(solution)/shard_map/reduce_scatter | solution.py:240
  8.6 1.3 copy-start.27
  9.9 4.8 copy-start.24
  14.7 11.9 %collective-permute-start.1 = (bf16[6,16,2048]{2,1,0:T(8,128)(2,1)S(1)}, bf16[6,16,2048]{2,1,0:T(8,128)(2,1)S(1)}, u32[]{:S(2)}, u32[]{:S(2)}) collective-permute-start(bf16[6,16,2048]{2,1,0:T(8,128)(2,1)S(1)} %bitcast.145), channel_id=1, source_target_pairs={{8,0},{16,8},{24,16},{0,24},{9,1},{17,9},{25,17},{1,25},{10,2},{18... | collective-permute-start | bytes 1179656 | tf_op jit(solution)/shard_map/ppermute | solution.py:23
  17.2 10.5 %collective-permute-start = (bf16[6,16,2048]{2,1,0:T(8,128)(2,1)S(1)}, bf16[6,16,2048]{2,1,0:T(8,128)(2,1)S(1)}, u32[]{:S(2)}, u32[]{:S(2)}) collective-permute-start(bf16[6,16,2048]{2,1,0:T(8,128)(2,1)S(1)} %bitcast.144), channel_id=1, source_target_pairs={{0,8},{8,16},{16,24},{24,0},{1,9},{9,17},{17,25},{25,1},{2,10},{10... | collective-permute-start | bytes 1179656 | tf_op jit(solution)/shard_map/ppermute | solution.py:21
  28.7 35.6 %collective-permute-start.3 = (bf16[28,6,2048]{2,0,1:T(8,128)(2,1)S(1)}, bf16[28,6,2048]{2,0,1:T(8,128)(2,1)S(1)}, u32[]{:S(2)}, u32[]{:S(2)}) collective-permute-start(bf16[28,6,2048]{2,0,1:T(8,128)(2,1)S(1)} %copy.33), channel_id=1, source_target_pairs={{1,0},{2,1},{3,2},{4,3},{5,4},{6,5},{7,6},{0,7},{9,8},{10,9},{11,1... | collective-permute-start | bytes 2064392 | tf_op jit(solution)/shard_map/ppermute | solution.py:23
  33.7 31.0 %collective-permute-start.2 = (bf16[28,6,2048]{2,0,1:T(8,128)(2,1)S(1)}, bf16[28,6,2048]{2,0,1:T(8,128)(2,1)S(1)}, u32[]{:S(2)}, u32[]{:S(2)}) collective-permute-start(bf16[28,6,2048]{2,0,1:T(8,128)(2,1)S(1)} %copy.32), channel_id=1, source_target_pairs={{0,1},{1,2},{2,3},{3,4},{4,5},{5,6},{6,7},{7,0},{8,9},{9,10},{10,1... | collective-permute-start | bytes 2064392 | tf_op jit(solution)/shard_map/ppermute | solution.py:21
  67.1 1.8 copy-start.10
  69.2 5.8 copy-start.30
  71.9 62.3 %collective-permute-start.4 = (bf16[2,6,28,2048]{3,0,2,1:T(2,128)(2,1)}, bf16[2,6,28,2048]{3,0,2,1:T(2,128)(2,1)}, u32[]{:S(2)}, u32[]{:S(2)}) collective-permute-start(bf16[2,6,28,2048]{3,0,2,1:T(2,128)(2,1)} %copy.36), channel_id=1, source_target_pairs={{0,4},{1,5},{2,6},{3,7},{4,0},{5,1},{6,2},{7,3},{8,12},{9,13},{10,... | collective-permute-start | bytes 4128776 | tf_op jit(solution)/shard_map/ppermute | solution.py:33
  79.2 124.8 %copy-start.14 = (bf16[4,64,16,64]{1,3,2,0:T(8,128)(2,1)}, bf16[4,64,16,64]{1,3,2,0:T(8,128)(2,1)S(1)}, u32[]{:S(2)}) copy-start(bf16[4,64,16,64]{1,3,2,0:T(8,128)(2,1)S(1)} %copy.51) | copy-start | bytes 1572868
  79.3 59.3 %copy-start.11 = (bf16[28,28,2048]{2,1,0:T(8,128)(2,1)S(1)}, bf16[28,28,2048]{2,1,0:T(8,128)(2,1)}, u32[]{:S(2)}) copy-start(bf16[28,28,2048]{2,1,0:T(8,128)(2,1)} %copy-done.10) | copy-start | bytes 9633796
  138.7 1.6 slice-start.1
  208.0 4.3 copy-start.1
  208.0 5.2 copy-start.8
  216.6 5.5 copy-start.18
  221.3 0.8 copy-start.16
  233.2 9.3 %copy-start.9 = (bf16[4,400,1024]{1,2,0:T(8,128)(2,1)S(1)}, bf16[4,400,1024]{1,2,0:T(8,128)(2,1)}, u32[]{:S(2)}) copy-start(bf16[4,400,1024]{1,2,0:T(8,128)(2,1)} %copy.64) | copy-start | bytes 9830404
  242.5 7.6 copy-start.15
  248.1 2.0 copy-start.4
  379.3 6.7 slice-start
  387.3 5.4 copy-start.17
  387.3 5.4 copy-start.19
  392.7 80.2 %collective-permute-start.5 = (bf16[2,6,28,2048]{3,0,2,1:T(2,128)(2,1)}, bf16[2,6,28,2048]{3,0,2,1:T(2,128)(2,1)}, u32[]{:S(2)}, u32[]{:S(2)}) collective-permute-start(bf16[2,6,28,2048]{3,0,2,1:T(2,128)(2,1)} %copy.56), channel_id=1, source_target_pairs={{0,4},{1,5},{2,6},{3,7},{4,0},{5,1},{6,2},{7,3},{8,12},{9,13},{10,... | collective-permute-start | bytes 4128776 | tf_op jit(solution)/shard_map/ppermute | solution.py:33
  395.4 375.3 %reduce-scatter.3.cloned.1.call-start = ((), (), s32[]{:S(2)}) async-start(), calls=%async_computation.2 | async-start | bytes 12976128 | tf_op jit(solution)/shard_map/reduce_scatter | solution.py:239
  484.2 20.6 %copy-start.2 = (bf16[28,28,2048]{2,1,0:T(8,128)(2,1)}, bf16[28,28,2048]{2,1,0:T(8,128)(2,1)S(1)}, u32[]{:S(2)}) copy-start(bf16[28,28,2048]{2,1,0:T(8,128)(2,1)S(1)} %convert_element_type.63) | copy-start | bytes 9633796
  484.4 16.3 %collective-permute-start.6 = (bf16[6,28,2048]{2,1,0:T(8,128)(2,1)S(1)}, bf16[6,28,2048]{2,1,0:T(8,128)(2,1)S(1)}, u32[]{:S(2)}, u32[]{:S(2)}) collective-permute-start(bf16[6,28,2048]{2,1,0:T(8,128)(2,1)S(1)} %get-tuple-element.104), channel_id=1, source_target_pairs={{0,8},{8,16},{16,24},{24,0},{1,9},{9,17},{17,25},{25,1},{2,10},{10... | collective-permute-start | bytes 2064392 | tf_op jit(solution)/shard_map/ppermute | solution.py:21
  484.5 18.8 %collective-permute-start.7 = (bf16[6,28,2048]{2,1,0:T(8,128)(2,1)S(1)}, bf16[6,28,2048]{2,1,0:T(8,128)(2,1)S(1)}, u32[]{:S(2)}, u32[]{:S(2)}) collective-permute-start(bf16[6,28,2048]{2,1,0:T(8,128)(2,1)S(1)} %get-tuple-element.105), channel_id=1, source_target_pairs={{8,0},{16,8},{24,16},{0,24},{9,1},{17,9},{25,17},{1,25},{10,2},{18... | collective-permute-start | bytes 2064392 | tf_op jit(solution)/shard_map/ppermute | solution.py:23
  503.3 0.9 copy-start.12
  504.2 10.7 %copy-start.6 = (bf16[4,400,1024]{1,2,0:T(8,128)(2,1)S(1)}, bf16[4,400,1024]{1,2,0:T(8,128)(2,1)}, u32[]{:S(2)}) copy-start(bf16[4,400,1024]{1,2,0:T(8,128)(2,1)} %copy.65) | copy-start | bytes 9830404
  504.8 10.1 %copy-start.5 = (bf16[4,16,64,400]{3,2,1,0:T(8,128)(2,1)S(1)}, bf16[4,16,64,400]{3,2,1,0:T(8,128)(2,1)}, u32[]{:S(2)}) copy-start(bf16[4,16,64,400]{3,2,1,0:T(8,128)(2,1)} %copy-done.4) | copy-start | bytes 9830404
  506.3 72.8 %collective-permute-start.9 = (bf16[40,6,2048]{2,0,1:T(8,128)(2,1)}, bf16[40,6,2048]{2,0,1:T(8,128)(2,1)}, u32[]{:S(2)}, u32[]{:S(2)}) collective-permute-start(bf16[40,6,2048]{2,0,1:T(8,128)(2,1)} %copy.59), channel_id=1, source_target_pairs={{1,0},{2,1},{3,2},{4,3},{5,4},{6,5},{7,6},{0,7},{9,8},{10,9},{11,1... | collective-permute-start | bytes 2949128 | tf_op jit(solution)/shard_map/ppermute | solution.py:23
  513.2 67.6 %collective-permute-start.8 = (bf16[40,6,2048]{2,0,1:T(8,128)(2,1)}, bf16[40,6,2048]{2,0,1:T(8,128)(2,1)}, u32[]{:S(2)}, u32[]{:S(2)}) collective-permute-start(bf16[40,6,2048]{2,0,1:T(8,128)(2,1)} %copy.58), channel_id=1, source_target_pairs={{0,1},{1,2},{2,3},{3,4},{4,5},{5,6},{6,7},{7,0},{8,9},{9,10},{10,1... | collective-permute-start | bytes 2949128 | tf_op jit(solution)/shard_map/ppermute | solution.py:21
  522.4 60.2 %copy-start.3 = (bf16[28,28,2048]{2,1,0:T(8,128)(2,1)S(1)}, bf16[28,28,2048]{2,1,0:T(8,128)(2,1)}, u32[]{:S(2)}) copy-start(bf16[28,28,2048]{2,1,0:T(8,128)(2,1)} %copy-done.2) | copy-start | bytes 9633796
  522.4 60.2 %copy-start.13 = (bf16[6,28,2048]{2,1,0:T(8,128)(2,1)S(1)}, bf16[6,28,2048]{2,1,0:T(8,128)(2,1)}, u32[]{:S(2)}) copy-start(bf16[6,28,2048]{2,1,0:T(8,128)(2,1)} %copy-done.12) | copy-start | bytes 2064388
  588.1 3.0 copy-start.7
  598.5 11.1 %copy-start.25 = (bf16[16,16,1024]{2,1,0:T(8,128)(2,1)S(1)}, bf16[16,16,1024]{2,1,0:T(8,128)(2,1)}, u32[]{:S(2)}) copy-start(bf16[16,16,1024]{2,1,0:T(8,128)(2,1)} %copy-done.24) | copy-start | bytes 1572868
  608.6 1.0 copy-start.22
  617.0 0.7 copy-start.28
  617.0 1.1 copy-start.21
  617.7 1.9 copy-start.29
  617.8 1.8 copy-start.23
  617.8 1.8 copy-start.26
  619.6 5.3 copy-start.20
Sparse Core Ops, SparseCore 0:
  395.6 178.6 reduce-scatter.4
  617.2 153.5 reduce-scatter.2
where the time goes:
time: 787 us; the launch traced here: 780 us
  waiting for transfers between devices  377 us (48%)
  local copies, waits for them, and re-layouts  227 us (29%)
  other arithmetic  89.4 us (11%)
  matrix products  52.5 us (7%)
  starting transfers between devices  18.8 us (2%)
  between operations  15.1 us (2%)
    reduce_scatter x1, waiting for transfers between devices, shards(): lax.psum_scatter(qkv_term, ('lat', 'lon'), scatter_dimension=0, tiled=True)  143 us
    ppermute x2, waiting for transfers between devices, shifted(): return lax.ppermute(value, axis, pairs)  121 us
    ppermute x4, waiting for transfers between devices, with_halo(): lax.ppermute(head, axis, [((i + 1) % count, i) for i in range(count)])  96.9 us
    concatenate x4, local copies, waits for them, and re-layouts, shards(): jnp.concatenate([grad_key_regions.reshape(tile_total, region_size, model_...  58 us
    gather x1, local copies, waits for them, and re-layouts, to_regions(): picked = framed[row_place, col_place]  42.9 us
    unnamed x4, other arithmetic  30.9 us
    unnamed x65, local copies, waits for them, and re-layouts  23.7 us
  transfers between devices with their start and end apart: 12, of which 9 were waited for; matrix products, arithmetic and copies ran while one was open for 12% of the time, Pallas kernels for 0%

commit v1 on v0

v1 whole, which is shorter than its diff:
```python
import jax
import jax.numpy as jnp
from jax import lax
from jax.experimental import pallas as pl
from jax.experimental.pallas import tpu as pltpu
from jax.sharding import PartitionSpec as P

H = 16
R = 6
SIDE_COLS = 8
PAIR = 128
TILE_ROWS = 8

epsilon = 1e-06
floor_score = -1e30

NT = (((1,), (1,)), ((), ()))


def dot(a, b, dims=(((1,), (0,)), ((), ()))):
    return lax.dot_general(a, b, dims, preferred_element_type=jnp.float32)


def attention_kernel(cols, row_count, q_ref, k_ref, v_ref, do_ref, o_ref, dq_ref, dk_ref, dv_ref, mask_ref):
    width = cols + 2 * SIDE_COLS
    queries = TILE_ROWS * cols
    keys = (TILE_ROWS + 2 * R) * width
    step = TILE_ROWS * width
    head = PAIR // 2

    @pl.when(pl.program_id(0) == 0)
    def _():
        key = lax.broadcasted_iota(jnp.int32, (keys, 2 * queries), 0)
        query = lax.rem(lax.broadcasted_iota(jnp.int32, (keys, 2 * queries), 1), queries)
        row_gap = lax.div(key, width) - lax.div(query, cols)
        place = lax.rem(key, width)
        place = jnp.where(
            place < cols,
            place,
            jnp.where(place < cols + SIDE_COLS, place - cols - SIDE_COLS, place - SIDE_COLS),
        )
        col_gap = place - lax.rem(query, cols)
        allowed = (row_gap >= 0) & (row_gap <= 2 * R) & (col_gap >= -R) & (col_gap <= R)
        mask_ref[...] = jnp.where(allowed, 0.0, floor_score)

    upper = lax.broadcasted_iota(jnp.int32, (2 * queries, PAIR), 0) < queries
    left = lax.broadcasted_iota(jnp.int32, (2 * queries, PAIR), 1) < head
    own = upper == left
    upper_t = lax.broadcasted_iota(jnp.int32, (PAIR, 2 * queries), 0) < head
    left_t = lax.broadcasted_iota(jnp.int32, (PAIR, 2 * queries), 1) < queries
    own_t = upper_t == left_t

    def paired(rows):
        twice = jnp.concatenate([rows, rows], axis=0)
        return jnp.where(own, twice, 0.0)

    def unpaired(both):
        picked = jnp.where(own_t, both, 0.0)
        return jnp.transpose(picked[:, :queries] + picked[:, queries:])

    k_all_t = jnp.transpose(k_ref[...])
    v_all_t = jnp.transpose(v_ref[...])
    dks, dvs = [], []
    for tile in range(row_count // TILE_ROWS):
        own_rows = slice(tile * queries, (tile + 1) * queries)
        own_keys = slice(tile * step, tile * step + keys)
        k = k_ref[own_keys, :]
        v = v_ref[own_keys, :]
        k_t = k_all_t[:, own_keys]
        v_t = v_all_t[:, own_keys]
        q32 = q_ref[own_rows, :].astype(jnp.float32) * (head ** (-0.5))
        do32 = do_ref[own_rows, :].astype(jnp.float32)
        q_pair = paired(q32).astype(jnp.bfloat16)
        do_pair32 = paired(do32)
        do_pair = do_pair32.astype(jnp.bfloat16)
        scores = dot(k, q_pair, NT) + mask_ref[...]
        highest = jnp.max(scores, axis=0, keepdims=True)
        raised = jnp.exp(scores - highest)
        chances = raised * (1.0 / jnp.sum(raised, axis=0, keepdims=True))
        chances_low = chances.astype(jnp.bfloat16)
        attended_t = dot(v_t, chances_low).astype(jnp.bfloat16).astype(jnp.float32)
        delta = jnp.sum(attended_t * jnp.transpose(do_pair32), axis=0, keepdims=True)
        o_ref[own_rows, :] = unpaired(attended_t).astype(jnp.bfloat16)
        grad_chances = dot(v, do_pair, NT)
        grad_scores = (chances * (grad_chances - delta)).astype(jnp.bfloat16)
        dq_ref[own_rows, :] = (unpaired(dot(k_t, grad_scores)) * (head ** (-0.5))).astype(
            jnp.bfloat16
        )
        dks.append(dot(grad_scores, q_pair))
        dvs.append(dot(chances_low, do_pair))

    for ref, parts in ((dk_ref, dks), (dv_ref, dvs)):
        for block in range(row_count // TILE_ROWS + (2 * R + TILE_ROWS - 1) // TILE_ROWS):
            low = block * step
            high = min(low + step, ref.shape[0])
            summed = None
            for tile, part in enumerate(parts):
                start = low - tile * step
                stop = min(high - tile * step, keys)
                if start < 0 or start >= keys:
                    continue
                piece = part[start:stop]
                if stop - start < high - low:
                    piece = jnp.concatenate(
                        [piece, jnp.zeros((high - low - stop + start, PAIR), jnp.float32)], axis=0
                    )
                summed = piece if summed is None else summed + piece
            ref[low:high, :] = summed.astype(jnp.bfloat16)


def attention(query, keyval, grad_attended, row_count, cols):
    cells, width_model = query.shape
    frame_cells = keyval.shape[0]
    pairs = width_model // PAIR
    keys = (TILE_ROWS + 2 * R) * (cols + 2 * SIDE_COLS)
    one = lambda rows, shift=0: pl.BlockSpec((rows, PAIR), lambda i: (0, i + shift))
    low = lambda rows: jax.ShapeDtypeStruct((rows, width_model), jnp.bfloat16)

    def kernel(*refs):
        attention_kernel(cols, row_count, *refs)

    return pl.pallas_call(
        kernel,
        grid=(pairs,),
        in_specs=[one(cells), one(frame_cells), one(frame_cells, pairs), one(cells)],
        out_specs=[one(cells), one(cells), one(frame_cells), one(frame_cells)],
        out_shape=[low(cells), low(cells), low(frame_cells), low(frame_cells)],
        scratch_shapes=[pltpu.VMEM((keys, 2 * TILE_ROWS * cols), jnp.float32)],
        compiler_params=pltpu.CompilerParams(vmem_limit_bytes=40 << 20),
        cost_estimate=pl.CostEstimate(
            flops=24 * cells * keys * width_model, bytes_accessed=16 << 20, transcendentals=cells * keys * H
        ),
    )(query, keyval, keyval, grad_attended)


def to_next(value, axis):
    count = lax.axis_size(axis)
    return lax.ppermute(value, axis, [(i, (i + 1) % count) for i in range(count)])


def to_previous(value, axis):
    count = lax.axis_size(axis)
    return lax.ppermute(value, axis, [((i + 1) % count, i) for i in range(count)])


def south_to_north(value):
    count = lax.axis_size("lat")
    return lax.ppermute(value, "lat", [(i + 1, i) for i in range(count - 1)])


def north_to_south(value):
    count = lax.axis_size("lat")
    return lax.ppermute(value, "lat", [(i, i + 1) for i in range(count - 1)])


def across_pole(value):
    lats = lax.axis_size("lat")
    lons = lax.axis_size("lon")
    pairs = [
        (lat * lons + lon, lat * lons + (lon + lons // 2) % lons)
        for lat in (0, lats - 1)
        for lon in range(lons)
    ]
    return lax.ppermute(value, ("lat", "lon"), pairs)


def shards(tokens, norm_gain, w_qkv, w_out, cotangent):
    rows, cols, width = tokens.shape
    lat_count = lax.axis_size("lat")
    device_count = lat_count * lax.axis_size("lon")
    at_north = lax.axis_index("lat") == 0
    at_south = lax.axis_index("lat") == lat_count - 1
    grad_scale = (rows * cols * device_count) ** (-0.5)
    side = SIDE_COLS

    west_mid = to_next(tokens[:, cols - side :], "lon")
    east_mid = to_previous(tokens[:, :side], "lon")
    top, bottom = tokens[:R], tokens[rows - R :]
    from_north = north_to_south(bottom)
    from_south = south_to_north(top)
    mirrored = across_pole(jnp.where(at_north, top, bottom)[::-1])
    top_in = jnp.where(at_north, mirrored, from_north)
    bottom_in = jnp.where(at_south, mirrored, from_south)
    edge = jnp.concatenate([top_in, bottom_in], axis=0)
    west_edge = to_next(edge[:, cols - side :], "lon")
    east_edge = to_previous(edge[:, :side], "lon")
    frame = jnp.concatenate(
        [
            jnp.concatenate([top_in, west_edge[:R], east_edge[:R]], axis=1),
            jnp.concatenate([tokens, west_mid, east_mid], axis=1),
            jnp.concatenate([bottom_in, west_edge[R:], east_edge[R:]], axis=1),
        ],
        axis=0,
    )
    frame_rows, frame_cols = frame.shape[:2]

    def normalise(cells):
        source = cells.astype(jnp.float32)
        inverse = lax.rsqrt(jnp.mean(source * source, axis=-1, keepdims=True) + epsilon)
        return (source * inverse * norm_gain).astype(jnp.bfloat16), source, inverse

    normed, source, inverse = normalise(tokens.reshape(-1, width))
    normed_frame = normalise(frame.reshape(-1, width))[0]
    w_query, w_keyval = w_qkv[:, :width], w_qkv[:, width:]
    query = dot(normed, w_query).astype(jnp.bfloat16)
    grad_flat = cotangent.reshape(-1, width)
    grad_attended = dot(grad_flat, w_out, NT).astype(jnp.bfloat16)
    keyval = dot(normed_frame, w_keyval).astype(jnp.bfloat16)
    attended, grad_query, grad_key, grad_value = attention(query, keyval, grad_attended, rows, cols)

    TN = (((0,), (0,)), ((), ()))
    qkv_term = jnp.concatenate(
        [
            dot(normed, grad_query, TN).astype(jnp.bfloat16),
            dot(normed_frame, grad_key, TN).astype(jnp.bfloat16),
            dot(normed_frame, grad_value, TN).astype(jnp.bfloat16),
        ],
        axis=1,
    )
    out_term = dot(attended, grad_flat, TN).astype(jnp.bfloat16)
    qkv_share = lax.psum_scatter(qkv_term, ("lat", "lon"), scatter_dimension=0, tiled=True)
    out_share = lax.psum_scatter(out_term, ("lat", "lon"), scatter_dimension=0, tiled=True)

    result = (dot(attended, w_out) + source).astype(jnp.bfloat16).reshape(rows, cols, width)

    spread = dot(grad_key, w_keyval[:, :width], NT) + dot(grad_value, w_keyval[:, width:], NT)
    spread = spread.reshape(frame_rows, frame_cols, width)
    strips = spread[:, cols:].astype(jnp.bfloat16)
    edges = jnp.concatenate([strips[:R], strips[R + rows :]], axis=0)
    west_edge_back = to_previous(edges[:, :side], "lon").astype(jnp.float32)
    east_edge_back = to_next(edges[:, side:], "lon").astype(jnp.float32)
    west_back = to_previous(strips[R : R + rows, :side], "lon").astype(jnp.float32)
    east_back = to_next(strips[R : R + rows, side:], "lon").astype(jnp.float32)
    edge_sum = jnp.concatenate([spread[:R, :cols], spread[R + rows :, :cols]], axis=0)
    edge_sum = edge_sum + jnp.concatenate([east_edge_back, west_edge_back], axis=1)
    edge_low = edge_sum.astype(jnp.bfloat16)
    top_out, bottom_out = edge_low[:R], edge_low[R:]
    to_north = south_to_north(top_out).astype(jnp.float32)
    to_south = north_to_south(bottom_out).astype(jnp.float32)
    pole_back = across_pole(jnp.where(at_north, top_out, bottom_out)[::-1]).astype(jnp.float32)
    top_back = jnp.where(at_north, pole_back, to_south)
    bottom_back = jnp.where(at_south, pole_back, to_north)
    grad_normed = spread[R : R + rows, :cols] + jnp.concatenate([east_back, west_back], axis=1)
    grad_normed = grad_normed + dot(grad_query, w_query, NT).reshape(rows, cols, width)
    gap = jnp.zeros((rows - R, cols, width), jnp.float32)
    grad_normed = grad_normed + jnp.concatenate([top_back, gap], axis=0)
    grad_normed = grad_normed + jnp.concatenate([gap, bottom_back], axis=0)

    scaled = norm_gain * grad_normed.reshape(-1, width)
    grad_input = (
        grad_flat.astype(jnp.float32)
        + inverse * scaled
        - source * inverse**3 * jnp.mean(source * scaled, axis=-1, keepdims=True)
    )
    grad_tokens = grad_input.astype(jnp.bfloat16).reshape(rows, cols, width)
    return (
        result,
        grad_tokens,
        qkv_share.astype(jnp.float32) * grad_scale,
        out_share.astype(jnp.float32) * grad_scale,
    )


def solution(mesh):
    placed = (P("lat", "lon", None), P(), P(), P(), P("lat", "lon", None))
    return jax.shard_map(
        shards,
        mesh=mesh,
        in_specs=placed,
        out_specs=(
            P("lat", "lon", None),
            P("lat", "lon", None),
            P(("lat", "lon"), None),
            P(("lat", "lon"), None),
        ),
        check_vma=False,
    )
```

time: 787 us -> 359 us (0.46)
  local copies, waits for them, and re-layouts: 227 us -> 19.9 us
  waiting for transfers between devices: 377 us -> 210 us
  other arithmetic: 89.4 us -> 29.9 us
  Pallas kernels: 0 us -> 21.2 us
  matrix products: 52.5 us -> 34.7 us
  starting transfers between devices: 18.8 us -> 27.7 us
    ppermute x10 -> x14, waiting for transfers between devices: 233 us -> 25.3 us  [the longest x4 15.7 us: to_previous(): lax.ppermute(value, axis, [((i + 1) % count, i) for i in range(count)])]
    unnamed x2 -> x3, waiting for transfers between devices: 0.03 us -> 117 us
    reduce_scatter x2 -> x1, waiting for transfers between devices: 143 us -> 67.6 us  [shards(): lax.psum_scatter(out_term, ('lat', 'lon'), scatter_dimension=0, tiled=True)]
    concatenate x5 -> x0, local copies, waits for them, and re-layouts: 58.1 us -> none  [the longest x4 58 us: shards(): jnp.concatenate([grad_key_regions.reshape(tile_total, region_size, model_...]
    gather x1 -> x0, local copies, waits for them, and re-layouts: 42.9 us -> none  [to_regions(): picked = framed[row_place, col_place]]
    unnamed x4 -> x0, other arithmetic: 30.9 us -> none
    slice x21 -> x6, local copies, waits for them, and re-layouts: 24.6 us -> 2 us  [the longest x1 1.07 us: shards(): west_mid = to_next(tokens[:, cols - side:], 'lon')]
    pallas_call x0 -> x1, Pallas kernels: none -> 21.2 us  [attention(): pl.pallas_call(kernel, grid=(pairs,), in_specs=[one(cells), one(frame_cel...]
  transfers between devices with their start and end apart: 12 -> 16, of which waited for: 9 -> 6; matrix products, arithmetic and copies ran while one was open for 12% -> 16% of each run, Pallas kernels for 0% -> 0%
where the time goes in v1:
time: 359 us; the launch traced here: 358 us
  waiting for transfers between devices  210 us (58%)
  matrix products  34.7 us (10%)
  other arithmetic  29.9 us (8%)
  starting transfers between devices  27.7 us (8%)
  Pallas kernels  21.2 us (6%)
  local copies, waits for them, and re-layouts  19.9 us (6%)
  between operations  14.5 us (4%)
    unnamed x3, waiting for transfers between devices  117 us
    reduce_scatter x1, waiting for transfers between devices, shards(): lax.psum_scatter(out_term, ('lat', 'lon'), scatter_dimension=0, tiled=True)  67.6 us
    dot_general x11, matrix products, dot(): return lax.dot_general(a, b, dims, preferred_element_type=jnp.float32)  34.7 us
    pallas_call x1, Pallas kernels, attention(): pl.pallas_call(kernel, grid=(pairs,), in_specs=[one(cells), one(frame_cel...  21.2 us
    unnamed x43, local copies, waits for them, and re-layouts  16.4 us
    ppermute x4, waiting for transfers between devices, to_previous(): lax.ppermute(value, axis, [((i + 1) % count, i) for i in range(count)])  15.7 us
    ppermute x4, starting transfers between devices, to_previous(): lax.ppermute(value, axis, [((i + 1) % count, i) for i in range(count)])  13.6 us
    concatenate x1, other arithmetic, shards(): jnp.concatenate([dot(normed, grad_query, TN).astype(jnp.bfloat16), dot(no...  13.5 us
  transfers between devices with their start and end apart: 16, of which 6 were waited for; matrix products, arithmetic and copies ran while one was open for 16% of the time, Pallas kernels for 0%

profile of v1, /device:TPU:0, one launch (start us, length us, event | category | flops | bytes accessed | tf_op | source)
XLA Modules:
  0.0 357.9 jit_solution(2929658484837783996)
XLA Ops:
  7.2 0.0 copy-start
  7.2 0.0 reduce-scatter.5.cloned.1.call-start
  7.3 2.0 fusion.41
  9.2 0.7 rev.6
  9.9 5.9 %collective-permute-start = (bf16[6,16,1024]{2,1,0:T(8,128)(2,1)}, bf16[6,16,1024]{2,1,0:T(8,128)(2,1)}, u32[]{:S(2)}, u32[]{:S(2)}) collective-permute-start(bf16[6,16,1024]{2,1,0:T(8,128)(2,1)} %rev.6), channel_id=1, source_target_pairs={{0,4},{1,5},{2,6},{3,7},{4,0},{5,1},{6,2},{7,3},{24,28},{25,29},{2... | collective-permute-start | bytes 589832 | tf_op jit(solution)/shard_map/ppermute | solution.py:164
  15.8 2.0 collective-permute-start.1
  17.8 1.3 collective-permute-start.2
  19.1 1.1 fusion.40
  20.2 2.4 collective-permute-start.6
  22.5 0.2 fusion.28
  22.7 0.6 multiply_multiply_fusion
  23.3 0.1 rsqrt.27
  23.4 0.2 fusion.27
  23.6 3.3 fusion.18.refs_0_
  27.0 1.1 broadcast_select_fusion.2
  28.1 4.8 %collective-permute-start.4 = (bf16[12,8,1024]{2,1,0:T(8,128)(2,1)S(1)}, bf16[12,8,1024]{2,1,0:T(8,128)(2,1)S(1)}, u32[]{:S(2)}, u32[]{:S(2)}) collective-permute-start(bf16[12,8,1024]{2,1,0:T(8,128)(2,1)S(1)} %get-tuple-element.41), channel_id=1, source_target_pairs={{1,0},{2,1},{3,2},{4,3},{5,4},{6,5},{7,6},{0,7},{9,8},{10,9},{11,1... | collective-permute-start | bytes 589832 | tf_op jit(solution)/shard_map/ppermute | solution.py:143
  32.9 1.5 convolution_convert_fusion.4.refs_3_
  34.4 4.7 %collective-permute-done.4 = bf16[12,8,1024]{2,1,0:T(8,128)(2,1)S(1)} collective-permute-done((bf16[12,8,1024]{2,1,0:T(8,128)(2,1)S(1)}, bf16[12,8,1024]{2,1,0:T(8,128)(2,1)S(1)}, u32[]{:S(2)}, u32[]{:S(2)}) %collective-permute-start.4) | collective-permute-done | bytes 196640 | tf_op jit(solution)/shard_map/ppermute | solution.py:143
  39.1 5.3 %collective-permute-done.3 = bf16[12,8,1024]{2,1,0:T(8,128)(2,1)S(1)} collective-permute-done((bf16[12,8,1024]{2,1,0:T(8,128)(2,1)S(1)}, bf16[12,8,1024]{2,1,0:T(8,128)(2,1)S(1)}, u32[]{:S(2)}, u32[]{:S(2)}) %collective-permute-start.3) | collective-permute-done | bytes 196640 | tf_op jit(solution)/shard_map/ppermute | solution.py:138
  44.4 2.9 multiply_reduce_fusion
  47.4 0.1 rsqrt.29
  47.4 2.4 fusion.3
  49.9 1.2 copy-done.15
  51.1 6.5 %fusion.4.refs_1_.refs_2_ = bf16[896,2048]{1,0:T(8,128)(2,1)S(1)} fusion(bf16[896,1024]{1,0:T(8,128)(2,1)S(1)} %fusion.3, bf16[1024,3072]{1,0:T(8,128)(2,1)} %param.7), kind=kOutput, calls=%fused_computation.7 | convolution fusion | flops 3759931392 | bytes 9699328 | tf_op jit(solution)/shard_map/dot_general | solution.py:21
  57.6 21.2 %shard_map.84 = (bf16[256,1024]{1,0:T(8,128)(2,1)S(1)}, bf16[256,1024]{1,0:T(8,128)(2,1)S(1)}, bf16[896,1024]{1,0:T(8,128)(2,1)S(1)}, bf16[896,1024]{1,0:T(8,128)(2,1)S(1)}) custom-call(bf16[256,1024]{1,0:T(8,128)(2,1)S(1)} %copy-done.2, bf16[896,2048]{1,0:T(8,128)(2,1)S(1)} %fusion.4.refs_1_.refs_2_, bf16[896,2048]{1,0:T(8,128)(2,1)S(1)} %fusion.4.refs_1_.refs_2_, ...), custom_call_target="tpu_custom_call" | custom-call | flops 4026531840 | bytes 16777216 | tf_op jit(solution)/shard_map/pallas_call | solution.py:122
  78.9 1.2 copy-done.3
  80.1 1.3 copy-done.5
  81.4 2.1 convolution_convert_fusion
  83.4 0.0 reduce-scatter.5.cloned.1.call-update
  83.4 0.2 reduce-scatter.7.cloned.1.call-start
  83.7 1.9 convolution_convert_fusion.3
  85.6 4.1 %convolution_convert_fusion.1 = bf16[1024,1024]{0,1:T(8,128)(2,1)S(1)} fusion(bf16[896,1024]{1,0:T(8,128)(2,1)} %copy-done.15, bf16[896,1024]{1,0:T(8,128)(2,1)S(1)} %copy-done.4), kind=kOutput, calls=%fused_computation.13 | convolution fusion | flops 1880096768 | bytes 5767168 | tf_op jit(solution)/shard_map/dot_general | solution.py:21
  89.7 2.4 convolution_convert_fusion.2
  92.2 13.5 %pad_maximum_fusion = bf16[1024,3072]{0,1:T(8,128)(2,1)} fusion(bf16[1024,1024]{0,1:T(8,128)(2,1)S(1)} %convolution_convert_fusion.1, bf16[1024,1024]{0,1:T(8,128)(2,1)S(1)} %convolution_convert_fusion.2, bf16[1024,1024]{0,1:T(8,128)(2,1)S(1)} %convolution_convert_fusion.3), kind=kLoop, calls=%fused_computation | loop fusion | flops 18874368 | bytes 12582912 | tf_op jit(solution)/shard_map/concatenate | solution.py:212
  105.7 8.6 %copy.11 = bf16[1024,3072]{1,0:T(8,128)(2,1)} copy(bf16[1024,3072]{0,1:T(8,128)(2,1)} %pad_maximum_fusion) | data formatting | bytes 12582912
  114.3 0.0 reduce-scatter.7.cloned.1.call-update
  114.3 4.4 %fusion.7 = f32[896,1024]{1,0:T(8,128)S(1)} fusion(bf16[896,1024]{1,0:T(8,128)(2,1)} %copy-done.3, bf16[1024,3072]{1,0:T(8,128)(2,1)} %param.7), kind=kOutput, calls=%fused_computation.8 | convolution fusion | flops 1879048192 | bytes 7602176 | tf_op jit(solution)/shard_map/dot_general | solution.py:21
  118.8 3.7 %fusion.15 = f32[896,1024]{1,0:T(8,128)S(1)} fusion(f32[896,1024]{1,0:T(8,128)S(1)} %fusion.7, bf16[896,1024]{1,0:T(8,128)(2,1)S(1)} %copy-done.7, bf16[1024,3072]{1,0:T(8,128)(2,1)} %param.7), kind=kOutput, calls=%fused_computation.21 | convolution fusion | flops 1879965696 | bytes 11272192 | tf_op jit(solution)/shard_map/dot_general | solution.py:21
  122.5 0.3 convert.7
  122.8 1.9 collective-permute-start.10
  124.7 0.2 collective-permute-start.9
  124.9 0.8 fusion.38
  125.7 4.5 %collective-permute-start.8 = (bf16[16,8,1024]{2,1,0:T(8,128)(2,1)}, bf16[16,8,1024]{2,1,0:T(8,128)(2,1)}, u32[]{:S(2)}, u32[]{:S(2)}) collective-permute-start(bf16[16,8,1024]{2,1,0:T(8,128)(2,1)} %get-tuple-element.27), channel_id=1, source_target_pairs={{1,0},{2,1},{3,2},{4,3},{5,4},{6,5},{7,6},{0,7},{9,8},{10,9},{11,1... | collective-permute-start | bytes 786440 | tf_op jit(solution)/shard_map/ppermute | solution.py:143
  130.3 3.3 fusion.11
  133.6 0.1 fusion.37
  133.7 11.0 %collective-permute-done.10 = bf16[12,8,1024]{2,1,0:T(8,128)(2,1)S(1)} collective-permute-done((bf16[12,8,1024]{2,1,0:T(8,128)(2,1)S(1)}, bf16[12,8,1024]{2,1,0:T(8,128)(2,1)S(1)}, u32[]{:S(2)}, u32[]{:S(2)}) %collective-permute-start.10) | collective-permute-done | bytes 196640 | tf_op jit(solution)/shard_map/ppermute | solution.py:143
  144.7 0.1 fusion.33
  144.8 0.7 fusion.42
  145.5 0.7 rev.7
  146.2 1.9 collective-permute-start.11
  148.1 1.3 collective-permute-start.12
  149.4 1.3 collective-permute-start.13
  150.7 1.5 fusion.21
  152.2 4.3 %collective-permute-done.11 = bf16[6,16,1024]{2,1,0:T(8,128)(2,1)S(1)} collective-permute-done((bf16[6,16,1024]{2,1,0:T(8,128)(2,1)}, bf16[6,16,1024]{2,1,0:T(8,128)(2,1)S(1)}, u32[]{:S(2)}, u32[]{:S(2)}) %collective-permute-start.11) | collective-permute-done | bytes 196640 | tf_op jit(solution)/shard_map/ppermute | solution.py:164
  156.5 0.1 convert_select_fusion.1
  156.7 1.8 fusion.32
  158.5 0.0 copy-done.19
  158.6 1.1 fusion.31
  159.7 67.6 %reduce-scatter.5.cloned.1.call-done = bf16[32,1024]{1,0:T(8,128)(2,1)} async-done(((bf16[1024,1024]{1,0:T(8,128)(2,1)}), bf16[32,1024]{1,0:T(8,128)(2,1)}) %reduce-scatter.5.cloned.1.call-update) | async-done | bytes 65552 | tf_op jit(solution)/shard_map/reduce_scatter | solution.py:222
  227.3 1.5 convert_multiply_fusion.4
  228.8 117.0 %reduce-scatter.7.cloned.1.call-done = bf16[32,3072]{1,0:T(8,128)(2,1)} async-done(((bf16[1024,3072]{1,0:T(8,128)(2,1)}), bf16[32,3072]{1,0:T(8,128)(2,1)}) %reduce-scatter.7.cloned.1.call-update) | async-done | bytes 196624
  345.8 1.3 copy.12
  347.1 1.3 convert_multiply_fusion
  348.4 2.6 copy.10
  (55 shorter events, 0.2 us)
Async XLA Ops:
  7.2 25.7 %copy-start = (bf16[1024,1024]{1,0:T(8,128)(2,1)S(1)}, bf16[1024,1024]{1,0:T(8,128)(2,1)}, u32[]{:S(2)}) copy-start(bf16[1024,1024]{1,0:T(8,128)(2,1)} %param.8) | copy-start | bytes 6291460
  7.2 15.4 %copy-start.8 = (bf16[16,16,1024]{2,1,0:T(8,128)(2,1)S(1)}, bf16[16,16,1024]{2,1,0:T(8,128)(2,1)}, u32[]{:S(2)}) copy-start(bf16[16,16,1024]{2,1,0:T(8,128)(2,1)} %param.5) | copy-start | bytes 1572868
  7.2 16.2 %copy-start.18 = (f32[1024]{0:T(1024)S(1)}, f32[1024]{0:T(1024)}, u32[]{:S(2)}) copy-start(f32[1024]{0:T(1024)} %param.6) | copy-start | bytes 12292
  7.2 220.1 %reduce-scatter.5.cloned.1.call-start = ((), (), s32[]{:S(2)}) async-start(), calls=%async_computation.2 | async-start | bytes 2162688 | tf_op jit(solution)/shard_map/reduce_scatter | solution.py:222
  9.9 17.1 %collective-permute-start = (bf16[6,16,1024]{2,1,0:T(8,128)(2,1)}, bf16[6,16,1024]{2,1,0:T(8,128)(2,1)}, u32[]{:S(2)}, u32[]{:S(2)}) collective-permute-start(bf16[6,16,1024]{2,1,0:T(8,128)(2,1)} %rev.6), channel_id=1, source_target_pairs={{0,4},{1,5},{2,6},{3,7},{4,0},{5,1},{6,2},{7,3},{24,28},{25,29},{2... | collective-permute-start | bytes 589832 | tf_op jit(solution)/shard_map/ppermute | solution.py:164
  15.8 11.1 %collective-permute-start.1 = (bf16[6,16,1024]{2,1,0:T(8,128)(2,1)}, bf16[6,16,1024]{2,1,0:T(8,128)(2,1)}, u32[]{:S(2)}, u32[]{:S(2)}) collective-permute-start(bf16[6,16,1024]{2,1,0:T(8,128)(2,1)} %get-tuple-element.32), channel_id=1, source_target_pairs={{0,8},{8,16},{16,24},{1,9},{9,17},{17,25},{2,10},{10,18},{18,26},{... | collective-permute-start | bytes 589832 | tf_op jit(solution)/shard_map/ppermute | solution.py:153
  17.8 9.1 %collective-permute-start.2 = (bf16[6,16,1024]{2,1,0:T(8,128)(2,1)}, bf16[6,16,1024]{2,1,0:T(8,128)(2,1)}, u32[]{:S(2)}, u32[]{:S(2)}) collective-permute-start(bf16[6,16,1024]{2,1,0:T(8,128)(2,1)} %get-tuple-element.34), channel_id=1, source_target_pairs={{8,0},{16,8},{24,16},{9,1},{17,9},{25,17},{10,2},{18,10},{26,18},{... | collective-permute-start | bytes 589832 | tf_op jit(solution)/shard_map/ppermute | solution.py:148
  20.2 24.3 %collective-permute-start.6 = (bf16[16,8,1024]{2,1,0:T(8,128)(2,1)S(1)}, bf16[16,8,1024]{2,1,0:T(8,128)(2,1)S(1)}, u32[]{:S(2)}, u32[]{:S(2)}) collective-permute-start(bf16[16,8,1024]{2,1,0:T(8,128)(2,1)S(1)} %get-tuple-element.31), channel_id=1, source_target_pairs={{1,0},{2,1},{3,2},{4,3},{5,4},{6,5},{7,6},{0,7},{9,8},{10,9},{11,1... | collective-permute-start | bytes 786440 | tf_op jit(solution)/shard_map/ppermute | solution.py:143
  22.5 21.9 %collective-permute-start.5 = (bf16[16,8,1024]{2,1,0:T(8,128)(2,1)S(1)}, bf16[16,8,1024]{2,1,0:T(8,128)(2,1)}, u32[]{:S(2)}, u32[]{:S(2)}) collective-permute-start(bf16[16,8,1024]{2,1,0:T(8,128)(2,1)S(1)} %get-tuple-element.30), channel_id=1, source_target_pairs={{0,1},{1,2},{2,3},{3,4},{4,5},{5,6},{6,7},{7,0},{8,9},{9,10},{10,1... | collective-permute-start | bytes 786440 | tf_op jit(solution)/shard_map/ppermute | solution.py:138
  23.6 3.3 copy-start.14
  23.6 9.2 %copy-start.11 = (bf16[16,16,1024]{2,1,0:T(8,128)(2,1)S(1)}, bf16[16,16,1024]{2,1,0:T(8,128)(2,1)}, u32[]{:S(2)}) copy-start(bf16[16,16,1024]{2,1,0:T(8,128)(2,1)} %param.9) | copy-start | bytes 1572868
  28.1 11.0 %collective-permute-start.4 = (bf16[12,8,1024]{2,1,0:T(8,128)(2,1)S(1)}, bf16[12,8,1024]{2,1,0:T(8,128)(2,1)S(1)}, u32[]{:S(2)}, u32[]{:S(2)}) collective-permute-start(bf16[12,8,1024]{2,1,0:T(8,128)(2,1)S(1)} %get-tuple-element.41), channel_id=1, source_target_pairs={{1,0},{2,1},{3,2},{4,3},{5,4},{6,5},{7,6},{0,7},{9,8},{10,9},{11,1... | collective-permute-start | bytes 589832 | tf_op jit(solution)/shard_map/ppermute | solution.py:143
  34.4 10.0 %collective-permute-start.3 = (bf16[12,8,1024]{2,1,0:T(8,128)(2,1)S(1)}, bf16[12,8,1024]{2,1,0:T(8,128)(2,1)S(1)}, u32[]{:S(2)}, u32[]{:S(2)}) collective-permute-start(bf16[12,8,1024]{2,1,0:T(8,128)(2,1)S(1)} %get-tuple-element.40), channel_id=1, source_target_pairs={{0,1},{1,2},{2,3},{3,4},{4,5},{5,6},{6,7},{7,0},{8,9},{9,10},{10,1... | collective-permute-start | bytes 589832 | tf_op jit(solution)/shard_map/ppermute | solution.py:138
  49.9 1.3 copy-start.15
  51.1 6.5 %copy-start.1 = (bf16[256,1024]{1,0:T(8,128)(2,1)S(1)}, bf16[256,1024]{1,0:T(8,128)(2,1)}, u32[]{:S(2)}) copy-start(bf16[256,1024]{1,0:T(8,128)(2,1)} %convolution_convert_fusion.4.refs_3_) | copy-start | bytes 1572868
  51.1 6.5 %copy-start.2 = (bf16[256,1024]{1,0:T(8,128)(2,1)S(1)}, bf16[256,1024]{1,0:T(8,128)(2,1)}, u32[]{:S(2)}) copy-start(bf16[256,1024]{1,0:T(8,128)(2,1)} %fusion.18.refs_0_) | copy-start | bytes 1572868
  57.6 23.7 %copy-start.12 = (bf16[16,16,1024]{2,1,0:T(8,128)(2,1)S(1)}, bf16[16,16,1024]{2,1,0:T(8,128)(2,1)}, u32[]{:S(2)}) copy-start(bf16[16,16,1024]{2,1,0:T(8,128)(2,1)} %param.9) | copy-start | bytes 1572868
  78.9 1.2 copy-start.3
  80.1 1.3 copy-start.5
  83.4 262.4 %reduce-scatter.7.cloned.1.call-start = ((), (), s32[]{:S(2)}) async-start(), calls=%async_computation.3 | async-start | bytes 6488064
  83.7 1.9 copy-start.4
  85.6 4.1 %copy-start.6 = (bf16[896,1024]{1,0:T(8,128)(2,1)S(1)}, bf16[896,1024]{1,0:T(8,128)(2,1)}, u32[]{:S(2)}) copy-start(bf16[896,1024]{1,0:T(8,128)(2,1)} %copy-done.5) | copy-start | bytes 5505028
  85.6 4.1 %copy-start.16 = (bf16[896,1024]{1,0:T(8,128)(2,1)S(1)}, bf16[896,1024]{1,0:T(8,128)(2,1)}, u32[]{:S(2)}) copy-start(bf16[896,1024]{1,0:T(8,128)(2,1)} %copy-done.15) | copy-start | bytes 5505028
  114.3 4.4 %copy-start.7 = (bf16[896,1024]{1,0:T(8,128)(2,1)S(1)}, bf16[896,1024]{1,0:T(8,128)(2,1)}, u32[]{:S(2)}) copy-start(bf16[896,1024]{1,0:T(8,128)(2,1)} %copy-done.5) | copy-start | bytes 5505028
  122.5 11.1 %copy-start.10 = (f32[896,1024]{1,0:T(8,128)}, f32[896,1024]{1,0:T(8,128)S(1)}, u32[]{:S(2)}) copy-start(f32[896,1024]{1,0:T(8,128)S(1)} %fusion.15) | copy-start | bytes 11010052
  122.8 21.8 %collective-permute-start.10 = (bf16[12,8,1024]{2,1,0:T(8,128)(2,1)S(1)}, bf16[12,8,1024]{2,1,0:T(8,128)(2,1)S(1)}, u32[]{:S(2)}, u32[]{:S(2)}) collective-permute-start(bf16[12,8,1024]{2,1,0:T(8,128)(2,1)S(1)} %get-tuple-element.39), channel_id=1, source_target_pairs={{1,0},{2,1},{3,2},{4,3},{5,4},{6,5},{7,6},{0,7},{9,8},{10,9},{11,1... | collective-permute-start | bytes 589832 | tf_op jit(solution)/shard_map/ppermute | solution.py:143
  124.7 19.9 %collective-permute-start.9 = (bf16[12,8,1024]{2,1,0:T(8,128)(2,1)S(1)}, bf16[12,8,1024]{2,1,0:T(8,128)(2,1)S(1)}, u32[]{:S(2)}, u32[]{:S(2)}) collective-permute-start(bf16[12,8,1024]{2,1,0:T(8,128)(2,1)S(1)} %get-tuple-element.38), channel_id=1, source_target_pairs={{0,1},{1,2},{2,3},{3,4},{4,5},{5,6},{6,7},{7,0},{8,9},{9,10},{10,1... | collective-permute-start | bytes 589832 | tf_op jit(solution)/shard_map/ppermute | solution.py:138
  125.7 30.9 %collective-permute-start.8 = (bf16[16,8,1024]{2,1,0:T(8,128)(2,1)}, bf16[16,8,1024]{2,1,0:T(8,128)(2,1)}, u32[]{:S(2)}, u32[]{:S(2)}) collective-permute-start(bf16[16,8,1024]{2,1,0:T(8,128)(2,1)} %get-tuple-element.27), channel_id=1, source_target_pairs={{1,0},{2,1},{3,2},{4,3},{5,4},{6,5},{7,6},{0,7},{9,8},{10,9},{11,1... | collective-permute-start | bytes 786440 | tf_op jit(solution)/shard_map/ppermute | solution.py:143
  130.3 26.4 %collective-permute-start.7 = (bf16[16,8,1024]{2,1,0:T(8,128)(2,1)}, bf16[16,8,1024]{2,1,0:T(8,128)(2,1)}, u32[]{:S(2)}, u32[]{:S(2)}) collective-permute-start(bf16[16,8,1024]{2,1,0:T(8,128)(2,1)} %get-tuple-element.26), channel_id=1, source_target_pairs={{0,1},{1,2},{2,3},{3,4},{4,5},{5,6},{6,7},{7,0},{8,9},{9,10},{10,1... | collective-permute-start | bytes 786440 | tf_op jit(solution)/shard_map/ppermute | solution.py:138
  133.6 17.1 %copy-start.9 = (bf16[16,16,1024]{2,1,0:T(8,128)(2,1)S(1)}, bf16[16,16,1024]{2,1,0:T(8,128)(2,1)}, u32[]{:S(2)}) copy-start(bf16[16,16,1024]{2,1,0:T(8,128)(2,1)} %param.5) | copy-start | bytes 1572868
  146.2 10.4 %collective-permute-start.11 = (bf16[6,16,1024]{2,1,0:T(8,128)(2,1)}, bf16[6,16,1024]{2,1,0:T(8,128)(2,1)S(1)}, u32[]{:S(2)}, u32[]{:S(2)}) collective-permute-start(bf16[6,16,1024]{2,1,0:T(8,128)(2,1)} %rev.7), channel_id=1, source_target_pairs={{0,4},{1,5},{2,6},{3,7},{4,0},{5,1},{6,2},{7,3},{24,28},{25,29},{2... | collective-permute-start | bytes 589832 | tf_op jit(solution)/shard_map/ppermute | solution.py:164
  148.1 8.4 %collective-permute-start.12 = (bf16[6,16,1024]{2,1,0:T(8,128)(2,1)}, bf16[6,16,1024]{2,1,0:T(8,128)(2,1)S(1)}, u32[]{:S(2)}, u32[]{:S(2)}) collective-permute-start(bf16[6,16,1024]{2,1,0:T(8,128)(2,1)} %get-tuple-element.35), channel_id=1, source_target_pairs={{0,8},{8,16},{16,24},{1,9},{9,17},{17,25},{2,10},{10,18},{18,26},{... | collective-permute-start | bytes 589832 | tf_op jit(solution)/shard_map/ppermute | solution.py:153
  149.4 7.1 %collective-permute-start.13 = (bf16[6,16,1024]{2,1,0:T(8,128)(2,1)S(1)}, bf16[6,16,1024]{2,1,0:T(8,128)(2,1)S(1)}, u32[]{:S(2)}, u32[]{:S(2)}) collective-permute-start(bf16[6,16,1024]{2,1,0:T(8,128)(2,1)S(1)} %get-tuple-element.37), channel_id=1, source_target_pairs={{8,0},{16,8},{24,16},{9,1},{17,9},{25,17},{10,2},{18,10},{26,18},{... | collective-permute-start | bytes 589832 | tf_op jit(solution)/shard_map/ppermute | solution.py:148
  150.7 5.9 %copy-start.17 = (f32[256,1024]{1,0:T(8,128)S(1)}, f32[256,1024]{1,0:T(8,128)}, u32[]{:S(2)}) copy-start(f32[256,1024]{1,0:T(8,128)} %fusion.11) | copy-start | bytes 3145732
  156.7 1.9 copy-start.13
  156.7 1.9 copy-start.19
Sparse Core Ops, SparseCore 0:
  83.6 143.7 reduce-scatter.4
  233.9 111.8 reduce-scatter.6

commit v2 on v1

--- a/solution.py
+++ b/solution.py
@@ -164,6 +164,25 @@
     return lax.ppermute(value, ("lat", "lon"), pairs)
 
 
+def halved(term, places, order):
+    places = list(places)
+    for axis, bit in order:
+        at = places.index((axis, bit))
+        places.pop(at)
+        outer, inner = 2**at, term.shape[0] // 2 ** (at + 1)
+        blocks = term.reshape(outer, 2, inner, term.shape[1])
+        upper = (lax.axis_index(axis) // 2**bit) % 2 == 1
+        first, second = blocks[:, 0], blocks[:, 1]
+        sent = jnp.where(upper, first, second)
+        kept = jnp.where(upper, second, first)
+        pairs = [(i, i ^ (1 << bit)) for i in range(lax.axis_size(axis))]
+        came = lax.ppermute(sent, axis, pairs)
+        total = kept.astype(jnp.float32) + came.astype(jnp.float32)
+        total = total.reshape(outer * inner, term.shape[1])
+        term = total if not places else total.astype(jnp.bfloat16)
+    return term, places
+
+
 def shards(tokens, norm_gain, w_qkv, w_out, cotangent):
     rows, cols, width = tokens.shape
     lat_count = lax.axis_size("lat")
@@ -209,17 +228,26 @@
     attended, grad_query, grad_key, grad_value = attention(query, keyval, grad_attended, rows, cols)
 
     TN = (((0,), (0,)), ((), ()))
-    qkv_term = jnp.concatenate(
-        [
-            dot(normed, grad_query, TN).astype(jnp.bfloat16),
-            dot(normed_frame, grad_key, TN).astype(jnp.bfloat16),
-            dot(normed_frame, grad_value, TN).astype(jnp.bfloat16),
-        ],
-        axis=1,
-    )
+    lat_bits = range(lat_count.bit_length() - 1)
+    lon_bits = range(lax.axis_size("lon").bit_length() - 1)
+    low_first = [("lat", bit) for bit in lat_bits] + [("lon", 0)]
+    low_first += [("lon", bit) for bit in reversed(lon_bits) if bit > 0]
+    lon_first = [("lat", 0), ("lon", 0), ("lon", len(lon_bits) - 1)]
+    lon_first += [("lat", bit) for bit in lat_bits if bit > 0]
+    lon_first += [("lon", bit) for bit in reversed(lon_bits) if 0 < bit < len(lon_bits) - 1]
+    places = [("lat", bit) for bit in reversed(lat_bits)]
+    places += [("lon", bit) for bit in reversed(lon_bits)]
+    split = len(lat_bits)
     out_term = dot(attended, grad_flat, TN).astype(jnp.bfloat16)
-    qkv_share = lax.psum_scatter(qkv_term, ("lat", "lon"), scatter_dimension=0, tiled=True)
-    out_share = lax.psum_scatter(out_term, ("lat", "lon"), scatter_dimension=0, tiled=True)
+    out_part, left_over = halved(out_term, places, low_first[:split])
+    query_term = dot(normed, grad_query, TN).astype(jnp.bfloat16)
+    query_part, left_over = halved(query_term, places, low_first[:split])
+    keyval_term = dot(normed_frame, jnp.concatenate([grad_key, grad_value], axis=1), TN)
+    keyval_share, none = halved(keyval_term.astype(jnp.bfloat16), places, lon_first)
+    pair_part = jnp.concatenate([query_part, out_part], axis=1)
+    pair_share, none = halved(pair_part, left_over, low_first[split:])
+    qkv_share = jnp.concatenate([pair_share[:, :width], keyval_share], axis=1)
+    out_share = pair_share[:, width:]
 
     result = (dot(attended, w_out) + source).astype(jnp.bfloat16).reshape(rows, cols, width)
 

time: 359 us -> 218 us (0.61)
  waiting for transfers between devices: 210 us -> 100 us
  local copies, waits for them, and re-layouts: 19.9 us -> 5.43 us
  between operations: 14.5 us -> 1.44 us
  starting transfers between devices: 27.7 us -> 39.3 us
  matrix products: 34.7 us -> 23.9 us
  other arithmetic: 29.9 us -> 26.1 us
    unnamed x3 -> x0, waiting for transfers between devices: 117 us -> none
    ppermute x0 -> x12, waiting for transfers between devices: none -> 82.6 us  [halved(): came = lax.ppermute(sent, axis, pairs)]
    reduce_scatter x1 -> x0, waiting for transfers between devices: 67.6 us -> none  [shards(): lax.psum_scatter(out_term, ('lat', 'lon'), scatter_dimension=0, tiled=True)]
    unnamed x43 -> x44, local copies, waits for them, and re-layouts: 16.4 us -> 0.81 us
    concatenate x1 -> x0, other arithmetic: 13.5 us -> none  [shards(): jnp.concatenate([dot(normed, grad_query, TN).astype(jnp.bfloat16), dot(no...]
    dot_general x11 -> x10, matrix products: 34.7 us -> 23.9 us  [dot(): return lax.dot_general(a, b, dims, preferred_element_type=jnp.float32)]
    ppermute x4, waiting for transfers between devices: 15.7 us -> 5.92 us  [to_previous(): lax.ppermute(value, axis, [((i + 1) % count, i) for i in range(count)])]
    convert_element_type x0 -> x10, other arithmetic: none -> 7.11 us  [halved(): term = total if not places else total.astype(jnp.bfloat16)]
  transfers between devices with their start and end apart: 16 -> 26, of which waited for: 6 -> 14; matrix products, arithmetic and copies ran while one was open for 16% -> 16% of each run, Pallas kernels for 0% -> 0%
where the time goes in v2:
time: 218 us
  waiting for transfers between devices  100 us (46%)
  starting transfers between devices  39.3 us (18%)
  other arithmetic  26.1 us (12%)
  matrix products  23.9 us (11%)
  Pallas kernels  21.2 us (10%)
  local copies, waits for them, and re-layouts  5.43 us (2%)
    ppermute x12, waiting for transfers between devices, halved(): came = lax.ppermute(sent, axis, pairs)  82.6 us
    dot_general x10, matrix products, dot(): return lax.dot_general(a, b, dims, preferred_element_type=jnp.float32)  23.9 us
    pallas_call x1, Pallas kernels, attention(): pl.pallas_call(kernel, grid=(pairs,), in_specs=[one(cells), one(frame_cel...  21.2 us
    ppermute x4, starting transfers between devices, to_previous(): lax.ppermute(value, axis, [((i + 1) % count, i) for i in range(count)])  16.9 us
    ppermute x4, waiting for transfers between devices, to_next(): lax.ppermute(value, axis, [(i, (i + 1) % count) for i in range(count)])  7.94 us
    convert_element_type x10, other arithmetic, halved(): term = total if not places else total.astype(jnp.bfloat16)  7.11 us
    ppermute x12, starting transfers between devices, halved(): came = lax.ppermute(sent, axis, pairs)  6.8 us
    ppermute x2, starting transfers between devices, across_pole(): return lax.ppermute(value, ('lat', 'lon'), pairs)  6.14 us
  transfers between devices with their start and end apart: 26, of which 14 were waited for; matrix products, arithmetic and copies ran while one was open for 16% of the time, Pallas kernels for 0%

profile of v2, /device:TPU:0, one launch (start us, length us, event | category | flops | bytes accessed | tf_op | source)
XLA Modules:
  0.0 217.8 jit_solution(4890016991240077347)
XLA Ops:
  0.7 1.9 fusion.68
  2.6 3.0 %collective-permute-start.5 = (bf16[16,8,1024]{2,1,0:T(8,128)(2,1)}, bf16[16,8,1024]{2,1,0:T(8,128)(2,1)}, u32[]{:S(2)}, u32[]{:S(2)}) collective-permute-start(bf16[16,8,1024]{2,1,0:T(8,128)(2,1)} %get-tuple-element.22), channel_id=1, source_target_pairs={{0,1},{1,2},{2,3},{3,4},{4,5},{5,6},{6,7},{7,0},{8,9},{9,10},{10,1... | collective-permute-start | bytes 786440 | tf_op jit(solution)/shard_map/ppermute | solution.py:138
  5.6 3.0 %collective-permute-start.6 = (bf16[16,8,1024]{2,1,0:T(8,128)(2,1)S(1)}, bf16[16,8,1024]{2,1,0:T(8,128)(2,1)}, u32[]{:S(2)}, u32[]{:S(2)}) collective-permute-start(bf16[16,8,1024]{2,1,0:T(8,128)(2,1)S(1)} %get-tuple-element.23), channel_id=1, source_target_pairs={{1,0},{2,1},{3,2},{4,3},{5,4},{6,5},{7,6},{0,7},{9,8},{10,9},{11,1... | collective-permute-start | bytes 786440 | tf_op jit(solution)/shard_map/ppermute | solution.py:143
  8.6 1.7 fusion.69
  10.3 0.7 rev.6
  11.0 2.8 %collective-permute-start = (bf16[6,16,1024]{2,1,0:T(8,128)(2,1)}, bf16[6,16,1024]{2,1,0:T(8,128)(2,1)S(1)}, u32[]{:S(2)}, u32[]{:S(2)}) collective-permute-start(bf16[6,16,1024]{2,1,0:T(8,128)(2,1)} %rev.6), channel_id=1, source_target_pairs={{0,4},{1,5},{2,6},{3,7},{4,0},{5,1},{6,2},{7,3},{24,28},{25,29},{2... | collective-permute-start | bytes 589832 | tf_op jit(solution)/shard_map/ppermute | solution.py:164
  13.9 2.0 collective-permute-start.1
  15.9 1.3 collective-permute-start.2
  17.5 0.6 multiply_multiply_fusion
  18.4 2.5 %fusion.25.refs_0_ = bf16[256,1024]{1,0:T(8,128)(2,1)S(1)} fusion(bf16[256,1024]{1,0:T(8,128)(2,1)S(1)} %fusion.44, bf16[1024,3072]{1,0:T(8,128)(2,1)} %param.7), kind=kOutput, calls=%fused_computation.37 | convolution fusion | flops 537133056 | bytes 3145728 | tf_op jit(solution)/shard_map/dot_general | solution.py:21
  21.2 1.0 broadcast_select_fusion.2
  22.2 0.5 collective-permute-start.3
  22.6 0.7 convolution_convert_fusion.3.refs_3_
  23.4 4.6 %collective-permute-start.4 = (bf16[12,8,1024]{2,1,0:T(8,128)(2,1)S(1)}, bf16[12,8,1024]{2,1,0:T(8,128)(2,1)S(1)}, u32[]{:S(2)}, u32[]{:S(2)}) collective-permute-start(bf16[12,8,1024]{2,1,0:T(8,128)(2,1)S(1)} %get-tuple-element.33), channel_id=1, source_target_pairs={{1,0},{2,1},{3,2},{4,3},{5,4},{6,5},{7,6},{0,7},{9,8},{10,9},{11,1... | collective-permute-start | bytes 589832 | tf_op jit(solution)/shard_map/ppermute | solution.py:143
  27.9 4.5 %collective-permute-done.3 = bf16[12,8,1024]{2,1,0:T(8,128)(2,1)S(1)} collective-permute-done((bf16[12,8,1024]{2,1,0:T(8,128)(2,1)S(1)}, bf16[12,8,1024]{2,1,0:T(8,128)(2,1)S(1)}, u32[]{:S(2)}, u32[]{:S(2)}) %collective-permute-start.3) | collective-permute-done | bytes 196640 | tf_op jit(solution)/shard_map/ppermute | solution.py:138
  32.5 3.3 %collective-permute-done.4 = bf16[12,8,1024]{2,1,0:T(8,128)(2,1)S(1)} collective-permute-done((bf16[12,8,1024]{2,1,0:T(8,128)(2,1)S(1)}, bf16[12,8,1024]{2,1,0:T(8,128)(2,1)S(1)}, u32[]{:S(2)}, u32[]{:S(2)}) %collective-permute-start.4) | collective-permute-done | bytes 196640 | tf_op jit(solution)/shard_map/ppermute | solution.py:143
  35.8 3.0 %multiply_reduce_fusion = (f32[28,32]{1,0:T(8,128)S(1)}, f32[28,32,1024]{2,1,0:T(8,128)}) fusion(bf16[6,8,1024]{2,1,0:T(8,128)(2,1)S(1)} %get-tuple-element.41, bf16[6,8,1024]{2,1,0:T(8,128)(2,1)S(1)} %get-tuple-element.39, bf16[6,16,1024]{2,1,0:T(8,128)(2,1)S(1)} %get-tuple-element.43, bf16[16,8,1024]{2,1,0:T(8,128)(2,1)} %collective-permute-done.6, ...), kind=kLoop, calls=%fused_computation.11 | loop fusion | flops 18349184 | bytes 5508608 | tf_op jit(solution)/shard_map/reduce_sum | solution.py:218
  38.9 2.6 %fusion.7 = bf16[896,1024]{1,0:T(8,128)(2,1)S(1)} fusion(f32[28,32,1024]{2,1,0:T(8,128)} %get-tuple-element.15, f32[1024]{0:T(1024)S(1)} %copy-done.18, f32[896]{0:T(1024)S(1)} %rsqrt.29), kind=kLoop, calls=%fused_computation.10 | loop fusion | flops 2752512 | bytes 5512704 | tf_op jit(solution)/shard_map/convert_element_type | solution.py:219
  41.5 6.5 %fusion.8.refs_1_.refs_2_ = bf16[896,2048]{1,0:T(8,128)(2,1)S(1)} fusion(bf16[896,1024]{1,0:T(8,128)(2,1)S(1)} %fusion.7, bf16[1024,3072]{1,0:T(8,128)(2,1)} %param.7), kind=kOutput, calls=%fused_computation.12 | convolution fusion | flops 3759931392 | bytes 9699328 | tf_op jit(solution)/shard_map/dot_general | solution.py:21
  48.0 21.2 %shard_map.84 = (bf16[256,1024]{1,0:T(8,128)(2,1)S(1)}, bf16[256,1024]{1,0:T(8,128)(2,1)S(1)}, bf16[896,1024]{1,0:T(8,128)(2,1)S(1)}, bf16[896,1024]{1,0:T(8,128)(2,1)S(1)}) custom-call(bf16[256,1024]{1,0:T(8,128)(2,1)S(1)} %fusion.25.refs_0_, bf16[896,2048]{1,0:T(8,128)(2,1)S(1)} %fusion.8.refs_1_.refs_2_, bf16[896,2048]{1,0:T(8,128)(2,1)S(1)} %fusion.8.refs_1_.refs_2_, ...), custom_call_target="tpu_custom_call" | custom-call | flops 4026531840 | bytes 16777216 | tf_op jit(solution)/shard_map/pallas_call | solution.py:122
  69.2 1.7 fusion.18
  71.0 0.7 convolution_convert_fusion.2
  72.0 0.7 convolution_convert_fusion.1
  72.8 0.4 copy-done.4
  73.2 1.5 fusion.28
  74.7 1.1 fusion.29
  75.9 1.1 select_bitcast_fusion.1
  77.0 0.4 collective-permute-start.16
  77.4 2.1 fusion.14
  79.5 5.2 %convolution_convert_fusion = bf16[1024,2048]{1,0:T(8,128)(2,1)S(1)} fusion(bf16[896,1024]{1,0:T(8,128)(2,1)S(1)} %fusion.7, bf16[896,1024]{1,0:T(8,128)(2,1)S(1)} %get-tuple-element.10, bf16[896,1024]{1,0:T(8,128)(2,1)S(1)} %get-tuple-element.9), kind=kOutput, calls=%fused_computation.4 | convolution fusion | flops 3767533568 | bytes 9699328 | tf_op jit(solution)/shard_map/dot_general | solution.py:21
  84.7 2.1 fusion.22
  86.8 0.3 convert.19
  87.2 4.7 %collective-permute-start.10 = (bf16[12,8,1024]{2,1,0:T(8,128)(2,1)S(1)}, bf16[12,8,1024]{2,1,0:T(8,128)(2,1)S(1)}, u32[]{:S(2)}, u32[]{:S(2)}) collective-permute-start(bf16[12,8,1024]{2,1,0:T(8,128)(2,1)S(1)} %get-tuple-element.31), channel_id=1, source_target_pairs={{1,0},{2,1},{3,2},{4,3},{5,4},{6,5},{7,6},{0,7},{9,8},{10,9},{11,1... | collective-permute-start | bytes 589832 | tf_op jit(solution)/shard_map/ppermute | solution.py:143
  91.9 1.5 select_bitcast_fusion
  93.5 3.4 %collective-permute-done.9 = bf16[12,8,1024]{2,1,0:T(8,128)(2,1)S(1)} collective-permute-done((bf16[12,8,1024]{2,1,0:T(8,128)(2,1)S(1)}, bf16[12,8,1024]{2,1,0:T(8,128)(2,1)S(1)}, u32[]{:S(2)}, u32[]{:S(2)}) %collective-permute-start.9) | collective-permute-done | bytes 196640 | tf_op jit(solution)/shard_map/ppermute | solution.py:138
  96.9 1.6 collective-permute-done.10
  98.6 0.7 fusion.70
  99.3 0.7 rev.7
  100.0 3.3 %collective-permute-start.11 = (bf16[6,16,1024]{2,1,0:T(8,128)(2,1)}, bf16[6,16,1024]{2,1,0:T(8,128)(2,1)S(1)}, u32[]{:S(2)}, u32[]{:S(2)}) collective-permute-start(bf16[6,16,1024]{2,1,0:T(8,128)(2,1)} %rev.7), channel_id=1, source_target_pairs={{0,4},{1,5},{2,6},{3,7},{4,0},{5,1},{6,2},{7,3},{24,28},{25,29},{2... | collective-permute-start | bytes 589832 | tf_op jit(solution)/shard_map/ppermute | solution.py:164
  103.3 1.3 collective-permute-start.12
  104.6 1.3 collective-permute-start.13
  105.9 1.1 fusion.66
  107.0 3.8 %collective-permute-done.11 = bf16[6,16,1024]{2,1,0:T(8,128)(2,1)S(1)} collective-permute-done((bf16[6,16,1024]{2,1,0:T(8,128)(2,1)}, bf16[6,16,1024]{2,1,0:T(8,128)(2,1)S(1)}, u32[]{:S(2)}, u32[]{:S(2)}) %collective-permute-start.11) | collective-permute-done | bytes 196640 | tf_op jit(solution)/shard_map/ppermute | solution.py:164
  110.9 4.6 %collective-permute-start.8 = (bf16[16,8,1024]{2,1,0:T(8,128)(2,1)S(1)}, bf16[16,8,1024]{2,1,0:T(8,128)(2,1)S(1)}, u32[]{:S(2)}, u32[]{:S(2)}) collective-permute-start(bf16[16,8,1024]{2,1,0:T(8,128)(2,1)S(1)} %get-tuple-element.19), channel_id=1, source_target_pairs={{1,0},{2,1},{3,2},{4,3},{5,4},{6,5},{7,6},{0,7},{9,8},{10,9},{11,1... | collective-permute-start | bytes 786440 | tf_op jit(solution)/shard_map/ppermute | solution.py:143
  115.6 2.0 fusion.31
  117.8 1.9 fusion.32
  119.8 2.0 collective-permute-start.17
  121.8 1.1 collective-permute-done.8
  122.9 1.6 fusion.49
  124.5 8.0 %collective-permute-done.15 = bf16[1,256,1024]{2,1,0:T(8,128)(2,1)S(1)} collective-permute-done((bf16[1,256,1024]{2,1,0:T(8,128)(2,1)S(1)}, bf16[1,256,1024]{2,1,0:T(8,128)(2,1)S(1)}, u32[]{:S(2)}, u32[]{:S(2)}) %collective-permute-start.15) | collective-permute-done | bytes 524320 | tf_op jit(solution)/shard_map/ppermute | solution.py:179
  132.8 10.6 %collective-permute-done.17 = bf16[1,256,1024]{2,1,0:T(8,128)(2,1)S(1)} collective-permute-done((bf16[1,256,1024]{2,1,0:T(8,128)(2,1)S(1)}, bf16[1,256,1024]{2,1,0:T(8,128)(2,1)S(1)}, u32[]{:S(2)}, u32[]{:S(2)}) %collective-permute-start.17) | collective-permute-done | bytes 524320 | tf_op jit(solution)/shard_map/ppermute | solution.py:179
  143.9 1.4 fusion
  145.4 2.1 collective-permute-start.22
  147.5 1.1 fusion.48
  148.6 10.1 %collective-permute-done.18 = bf16[4,32,2048]{2,1,0:T(8,128)(2,1)S(1)} collective-permute-done((bf16[4,32,2048]{2,1,0:T(8,128)(2,1)S(1)}, bf16[4,32,2048]{2,1,0:T(8,128)(2,1)S(1)}, u32[]{:S(2)}, u32[]{:S(2)}) %collective-permute-start.18) | collective-permute-done | bytes 524320 | tf_op jit(solution)/shard_map/ppermute | solution.py:179
  159.0 20.8 %collective-permute-done.22 = bf16[8,32,2048]{2,1,0:T(8,128)(2,1)S(1)} collective-permute-done((bf16[8,32,2048]{2,1,0:T(8,128)(2,1)S(1)}, bf16[8,32,2048]{2,1,0:T(8,128)(2,1)S(1)}, u32[]{:S(2)}, u32[]{:S(2)}) %collective-permute-start.22) | collective-permute-done | bytes 1048608 | tf_op jit(solution)/shard_map/ppermute | solution.py:179
  179.8 0.5 fusion.11
  180.7 1.1 collective-permute-start.20
  181.8 21.4 %collective-permute-done.23 = bf16[2,64,2048]{2,1,0:T(8,128)(2,1)S(1)} collective-permute-done((bf16[2,64,2048]{2,1,0:T(8,128)(2,1)S(1)}, bf16[2,64,2048]{2,1,0:T(8,128)(2,1)S(1)}, u32[]{:S(2)}, u32[]{:S(2)}) %collective-permute-start.23) | collective-permute-done | bytes 524320 | tf_op jit(solution)/shard_map/ppermute | solution.py:179
  203.5 0.8 collective-permute-start.24
  204.3 7.5 %collective-permute-done.24 = bf16[1,64,2048]{2,1,0:T(8,128)(2,1)S(1)} collective-permute-done((bf16[1,64,2048]{2,1,0:T(8,128)(2,1)S(1)}, bf16[1,64,2048]{2,1,0:T(8,128)(2,1)S(1)}, u32[]{:S(2)}, u32[]{:S(2)}) %collective-permute-start.24) | collective-permute-done | bytes 262176 | tf_op jit(solution)/shard_map/ppermute | solution.py:179
  212.0 0.7 slice_multiply_fusion
  212.7 4.3 %collective-permute-done.25 = bf16[1,32,2048]{2,1,0:T(8,128)(2,1)S(1)} collective-permute-done((bf16[1,32,2048]{2,1,0:T(8,128)(2,1)S(1)}, bf16[1,32,2048]{2,1,0:T(8,128)(2,1)S(1)}, u32[]{:S(2)}, u32[]{:S(2)}) %collective-permute-start.25) | collective-permute-done | bytes 131104 | tf_op jit(solution)/shard_map/ppermute | solution.py:179
  217.0 0.8 maximum_multiply_fusion
  (97 shorter events, 4.0 us)
Async XLA Ops:
  0.6 22.0 %copy-start = (bf16[1024,1024]{1,0:T(8,128)(2,1)S(1)}, bf16[1024,1024]{1,0:T(8,128)(2,1)}, u32[]{:S(2)}) copy-start(bf16[1024,1024]{1,0:T(8,128)(2,1)} %param.8) | copy-start | bytes 6291460
  0.6 16.6 %copy-start.2 = (bf16[16,16,1024]{2,1,0:T(8,128)(2,1)S(1)}, bf16[16,16,1024]{2,1,0:T(8,128)(2,1)}, u32[]{:S(2)}) copy-start(bf16[16,16,1024]{2,1,0:T(8,128)(2,1)} %param.5) | copy-start | bytes 1572868
  0.7 17.5 %copy-start.18 = (f32[1024]{0:T(1024)S(1)}, f32[1024]{0:T(1024)}, u32[]{:S(2)}) copy-start(f32[1024]{0:T(1024)} %param.6) | copy-start | bytes 12292
  2.6 33.2 %collective-permute-start.5 = (bf16[16,8,1024]{2,1,0:T(8,128)(2,1)}, bf16[16,8,1024]{2,1,0:T(8,128)(2,1)}, u32[]{:S(2)}, u32[]{:S(2)}) collective-permute-start(bf16[16,8,1024]{2,1,0:T(8,128)(2,1)} %get-tuple-element.22), channel_id=1, source_target_pairs={{0,1},{1,2},{2,3},{3,4},{4,5},{5,6},{6,7},{7,0},{8,9},{9,10},{10,1... | collective-permute-start | bytes 786440 | tf_op jit(solution)/shard_map/ppermute | solution.py:138
  5.6 30.2 %collective-permute-start.6 = (bf16[16,8,1024]{2,1,0:T(8,128)(2,1)S(1)}, bf16[16,8,1024]{2,1,0:T(8,128)(2,1)}, u32[]{:S(2)}, u32[]{:S(2)}) collective-permute-start(bf16[16,8,1024]{2,1,0:T(8,128)(2,1)S(1)} %get-tuple-element.23), channel_id=1, source_target_pairs={{1,0},{2,1},{3,2},{4,3},{5,4},{6,5},{7,6},{0,7},{9,8},{10,9},{11,1... | collective-permute-start | bytes 786440 | tf_op jit(solution)/shard_map/ppermute | solution.py:143
  11.0 10.1 %collective-permute-start = (bf16[6,16,1024]{2,1,0:T(8,128)(2,1)}, bf16[6,16,1024]{2,1,0:T(8,128)(2,1)S(1)}, u32[]{:S(2)}, u32[]{:S(2)}) collective-permute-start(bf16[6,16,1024]{2,1,0:T(8,128)(2,1)} %rev.6), channel_id=1, source_target_pairs={{0,4},{1,5},{2,6},{3,7},{4,0},{5,1},{6,2},{7,3},{24,28},{25,29},{2... | collective-permute-start | bytes 589832 | tf_op jit(solution)/shard_map/ppermute | solution.py:164
  13.9 7.3 %collective-permute-start.1 = (bf16[6,16,1024]{2,1,0:T(8,128)(2,1)}, bf16[6,16,1024]{2,1,0:T(8,128)(2,1)}, u32[]{:S(2)}, u32[]{:S(2)}) collective-permute-start(bf16[6,16,1024]{2,1,0:T(8,128)(2,1)} %get-tuple-element.24), channel_id=1, source_target_pairs={{0,8},{8,16},{16,24},{1,9},{9,17},{17,25},{2,10},{10,18},{18,26},{... | collective-permute-start | bytes 589832 | tf_op jit(solution)/shard_map/ppermute | solution.py:153
  15.9 5.3 %collective-permute-start.2 = (bf16[6,16,1024]{2,1,0:T(8,128)(2,1)S(1)}, bf16[6,16,1024]{2,1,0:T(8,128)(2,1)}, u32[]{:S(2)}, u32[]{:S(2)}) collective-permute-start(bf16[6,16,1024]{2,1,0:T(8,128)(2,1)S(1)} %get-tuple-element.26), channel_id=1, source_target_pairs={{8,0},{16,8},{24,16},{9,1},{17,9},{25,17},{10,2},{18,10},{26,18},{... | collective-permute-start | bytes 589832 | tf_op jit(solution)/shard_map/ppermute | solution.py:148
  18.4 2.6 %copy-start.15 = (bf16[256,1024]{1,0:T(8,128)(2,1)}, bf16[256,1024]{1,0:T(8,128)(2,1)S(1)}, u32[]{:S(2)}) copy-start(bf16[256,1024]{1,0:T(8,128)(2,1)S(1)} %fusion.44) | copy-start | bytes 1572868
  18.4 4.3 %copy-start.13 = (bf16[16,16,1024]{2,1,0:T(8,128)(2,1)S(1)}, bf16[16,16,1024]{2,1,0:T(8,128)(2,1)}, u32[]{:S(2)}) copy-start(bf16[16,16,1024]{2,1,0:T(8,128)(2,1)} %param.9) | copy-start | bytes 1572868
  22.2 10.3 %collective-permute-start.3 = (bf16[12,8,1024]{2,1,0:T(8,128)(2,1)S(1)}, bf16[12,8,1024]{2,1,0:T(8,128)(2,1)S(1)}, u32[]{:S(2)}, u32[]{:S(2)}) collective-permute-start(bf16[12,8,1024]{2,1,0:T(8,128)(2,1)S(1)} %get-tuple-element.32), channel_id=1, source_target_pairs={{0,1},{1,2},{2,3},{3,4},{4,5},{5,6},{6,7},{7,0},{8,9},{9,10},{10,1... | collective-permute-start | bytes 589832 | tf_op jit(solution)/shard_map/ppermute | solution.py:138
  22.6 13.2 %copy-start.3 = (bf16[16,16,1024]{2,1,0:T(8,128)(2,1)S(1)}, bf16[16,16,1024]{2,1,0:T(8,128)(2,1)}, u32[]{:S(2)}) copy-start(bf16[16,16,1024]{2,1,0:T(8,128)(2,1)} %param.5) | copy-start | bytes 1572868
  23.4 12.4 %collective-permute-start.4 = (bf16[12,8,1024]{2,1,0:T(8,128)(2,1)S(1)}, bf16[12,8,1024]{2,1,0:T(8,128)(2,1)S(1)}, u32[]{:S(2)}, u32[]{:S(2)}) collective-permute-start(bf16[12,8,1024]{2,1,0:T(8,128)(2,1)S(1)} %get-tuple-element.33), channel_id=1, source_target_pairs={{1,0},{2,1},{3,2},{4,3},{5,4},{6,5},{7,6},{0,7},{9,8},{10,9},{11,1... | collective-permute-start | bytes 589832 | tf_op jit(solution)/shard_map/ppermute | solution.py:143
  38.9 30.3 %slice-start = ((s8[6291456]{0:T(1024)(128)(4,1)}), s8[4194304]{0:T(1024)(128)(4,1)S(1)}, s32[]{:S(2)}) async-start(s8[6291456]{0:T(1024)(128)(4,1)} %bitcast.226), calls=%async_computation | async-start | bytes 8388608
  41.5 27.8 %slice-start.1 = ((s8[6291456]{0:T(1024)(128)(4,1)}), s8[2097152]{0:T(1024)(128)(4,1)S(1)}, s32[]{:S(2)}) async-start(s8[6291456]{0:T(1024)(128)(4,1)} %bitcast.226), calls=%async_computation.1 | async-start | bytes 4194304
  69.2 1.8 copy-start.16
  71.0 1.0 copy-start.14
  71.7 3.0 %copy-start.7 = (bf16[1024,1024]{1,0:T(8,128)(2,1)}, bf16[1024,1024]{1,0:T(8,128)(2,1)S(1)}, u32[]{:S(2)}) copy-start(bf16[1024,1024]{1,0:T(8,128)(2,1)S(1)} %convolution_convert_fusion.2) | copy-start | bytes 6291460
  71.7 1.5 copy-start.4
  72.8 3.1 %copy-start.5 = (bf16[1024,1024]{1,0:T(8,128)(2,1)}, bf16[1024,1024]{1,0:T(8,128)(2,1)S(1)}, u32[]{:S(2)}) copy-start(bf16[1024,1024]{1,0:T(8,128)(2,1)S(1)} %convolution_convert_fusion.1) | copy-start | bytes 6291460
  75.8 39.9 %collective-permute-start.14 = (bf16[2,256,1024]{2,1,0:T(8,128)(2,1)}, bf16[2,256,1024]{2,1,0:T(8,128)(2,1)}, u32[]{:S(2)}, u32[]{:S(2)}) collective-permute-start(bf16[2,256,1024]{2,1,0:T(8,128)(2,1)} %fusion.29), channel_id=1, source_target_pairs={{0,8},{8,0},{16,24},{24,16},{1,9},{9,1},{17,25},{25,17},{2,10},{10... | collective-permute-start | bytes 3145736 | tf_op jit(solution)/shard_map/ppermute | solution.py:179
  77.0 40.8 %collective-permute-start.16 = (bf16[2,256,1024]{2,1,0:T(8,128)(2,1)}, bf16[2,256,1024]{2,1,0:T(8,128)(2,1)}, u32[]{:S(2)}, u32[]{:S(2)}) collective-permute-start(bf16[2,256,1024]{2,1,0:T(8,128)(2,1)} %select_bitcast_fusion.1), channel_id=1, source_target_pairs={{0,8},{8,0},{16,24},{24,16},{1,9},{9,1},{17,25},{25,17},{2,10},{10... | collective-permute-start | bytes 3145736 | tf_op jit(solution)/shard_map/ppermute | solution.py:179
  84.7 7.3 %copy-start.9 = (bf16[1024,2048]{1,0:T(8,128)(2,1)}, bf16[1024,2048]{1,0:T(8,128)(2,1)S(1)}, u32[]{:S(2)}) copy-start(bf16[1024,2048]{1,0:T(8,128)(2,1)S(1)} %convolution_convert_fusion) | copy-start | bytes 12582916
  86.8 6.7 %copy-start.11 = (f32[896,1024]{1,0:T(8,128)}, f32[896,1024]{1,0:T(8,128)S(1)}, u32[]{:S(2)}) copy-start(f32[896,1024]{1,0:T(8,128)S(1)} %fusion.22) | copy-start | bytes 11010052
  87.1 6.4 %copy-start.12 = (bf16[28,32,1024]{2,1,0:T(8,128)(2,1)}, bf16[28,32,1024]{2,1,0:T(8,128)(2,1)S(1)}, u32[]{:S(2)}) copy-start(bf16[28,32,1024]{2,1,0:T(8,128)(2,1)S(1)} %convert.19) | copy-start | bytes 5505028
  87.2 9.8 %collective-permute-start.9 = (bf16[12,8,1024]{2,1,0:T(8,128)(2,1)S(1)}, bf16[12,8,1024]{2,1,0:T(8,128)(2,1)S(1)}, u32[]{:S(2)}, u32[]{:S(2)}) collective-permute-start(bf16[12,8,1024]{2,1,0:T(8,128)(2,1)S(1)} %get-tuple-element.30), channel_id=1, source_target_pairs={{0,1},{1,2},{2,3},{3,4},{4,5},{5,6},{6,7},{7,0},{8,9},{9,10},{10,1... | collective-permute-start | bytes 589832 | tf_op jit(solution)/shard_map/ppermute | solution.py:138
  87.2 11.3 %collective-permute-start.10 = (bf16[12,8,1024]{2,1,0:T(8,128)(2,1)S(1)}, bf16[12,8,1024]{2,1,0:T(8,128)(2,1)S(1)}, u32[]{:S(2)}, u32[]{:S(2)}) collective-permute-start(bf16[12,8,1024]{2,1,0:T(8,128)(2,1)S(1)} %get-tuple-element.31), channel_id=1, source_target_pairs={{1,0},{2,1},{3,2},{4,3},{5,4},{6,5},{7,6},{0,7},{9,8},{10,9},{11,1... | collective-permute-start | bytes 589832 | tf_op jit(solution)/shard_map/ppermute | solution.py:143
  98.6 17.0 %copy-start.8 = (bf16[1024,1024]{1,0:T(8,128)(2,1)S(1)}, bf16[1024,1024]{1,0:T(8,128)(2,1)}, u32[]{:S(2)}) copy-start(bf16[1024,1024]{1,0:T(8,128)(2,1)} %copy-done.7) | copy-start | bytes 6291460
  100.0 10.8 %collective-permute-start.11 = (bf16[6,16,1024]{2,1,0:T(8,128)(2,1)}, bf16[6,16,1024]{2,1,0:T(8,128)(2,1)S(1)}, u32[]{:S(2)}, u32[]{:S(2)}) collective-permute-start(bf16[6,16,1024]{2,1,0:T(8,128)(2,1)} %rev.7), channel_id=1, source_target_pairs={{0,4},{1,5},{2,6},{3,7},{4,0},{5,1},{6,2},{7,3},{24,28},{25,29},{2... | collective-permute-start | bytes 589832 | tf_op jit(solution)/shard_map/ppermute | solution.py:164
  103.3 7.6 %collective-permute-start.12 = (bf16[6,16,1024]{2,1,0:T(8,128)(2,1)}, bf16[6,16,1024]{2,1,0:T(8,128)(2,1)S(1)}, u32[]{:S(2)}, u32[]{:S(2)}) collective-permute-start(bf16[6,16,1024]{2,1,0:T(8,128)(2,1)} %get-tuple-element.27), channel_id=1, source_target_pairs={{0,8},{8,16},{16,24},{1,9},{9,17},{17,25},{2,10},{10,18},{18,26},{... | collective-permute-start | bytes 589832 | tf_op jit(solution)/shard_map/ppermute | solution.py:153
  104.6 10.9 %collective-permute-start.13 = (bf16[6,16,1024]{2,1,0:T(8,128)(2,1)S(1)}, bf16[6,16,1024]{2,1,0:T(8,128)(2,1)S(1)}, u32[]{:S(2)}, u32[]{:S(2)}) collective-permute-start(bf16[6,16,1024]{2,1,0:T(8,128)(2,1)S(1)} %get-tuple-element.29), channel_id=1, source_target_pairs={{8,0},{16,8},{24,16},{9,1},{17,9},{25,17},{10,2},{18,10},{26,18},{... | collective-permute-start | bytes 589832 | tf_op jit(solution)/shard_map/ppermute | solution.py:148
  110.8 11.0 %collective-permute-start.7 = (bf16[16,8,1024]{2,1,0:T(8,128)(2,1)S(1)}, bf16[16,8,1024]{2,1,0:T(8,128)(2,1)S(1)}, u32[]{:S(2)}, u32[]{:S(2)}) collective-permute-start(bf16[16,8,1024]{2,1,0:T(8,128)(2,1)S(1)} %get-tuple-element.18), channel_id=1, source_target_pairs={{0,1},{1,2},{2,3},{3,4},{4,5},{5,6},{6,7},{7,0},{8,9},{9,10},{10,1... | collective-permute-start | bytes 786440 | tf_op jit(solution)/shard_map/ppermute | solution.py:138
  110.9 12.0 %collective-permute-start.8 = (bf16[16,8,1024]{2,1,0:T(8,128)(2,1)S(1)}, bf16[16,8,1024]{2,1,0:T(8,128)(2,1)S(1)}, u32[]{:S(2)}, u32[]{:S(2)}) collective-permute-start(bf16[16,8,1024]{2,1,0:T(8,128)(2,1)S(1)} %get-tuple-element.19), channel_id=1, source_target_pairs={{1,0},{2,1},{3,2},{4,3},{5,4},{6,5},{7,6},{0,7},{9,8},{10,9},{11,1... | collective-permute-start | bytes 786440 | tf_op jit(solution)/shard_map/ppermute | solution.py:143
  115.5 28.3 %collective-permute-start.21 = (bf16[2,256,2048]{2,1,0:T(8,128)(2,1)}, bf16[2,256,2048]{2,1,0:T(8,128)(2,1)S(1)}, u32[]{:S(2)}, u32[]{:S(2)}) collective-permute-start(bf16[2,256,2048]{2,1,0:T(8,128)(2,1)} %select_bitcast_fusion), channel_id=1, source_target_pairs={{0,8},{8,0},{16,24},{24,16},{1,9},{9,1},{17,25},{25,17},{2,10},{10... | collective-permute-start | bytes 6291464 | tf_op jit(solution)/shard_map/ppermute | solution.py:179
  115.6 2.2 %copy-start.6 = (bf16[1024,1024]{1,0:T(8,128)(2,1)S(1)}, bf16[1024,1024]{1,0:T(8,128)(2,1)}, u32[]{:S(2)}) copy-start(bf16[1024,1024]{1,0:T(8,128)(2,1)} %copy-done.5) | copy-start | bytes 6291460
  117.7 5.2 %copy-start.17 = (f32[256,1024]{1,0:T(8,128)S(1)}, f32[256,1024]{1,0:T(8,128)}, u32[]{:S(2)}) copy-start(f32[256,1024]{1,0:T(8,128)} %fusion.18) | copy-start | bytes 3145732
  117.7 14.8 %collective-permute-start.15 = (bf16[1,256,1024]{2,1,0:T(8,128)(2,1)S(1)}, bf16[1,256,1024]{2,1,0:T(8,128)(2,1)S(1)}, u32[]{:S(2)}, u32[]{:S(2)}) collective-permute-start(bf16[1,256,1024]{2,1,0:T(8,128)(2,1)S(1)} %select_bitcast_fusion.3), channel_id=1, source_target_pairs={{0,16},{8,24},{16,0},{24,8},{1,17},{9,25},{17,1},{25,9},{2,18},{10... | collective-permute-start | bytes 1572872 | tf_op jit(solution)/shard_map/ppermute | solution.py:179
  119.8 23.5 %collective-permute-start.17 = (bf16[1,256,1024]{2,1,0:T(8,128)(2,1)S(1)}, bf16[1,256,1024]{2,1,0:T(8,128)(2,1)S(1)}, u32[]{:S(2)}, u32[]{:S(2)}) collective-permute-start(bf16[1,256,1024]{2,1,0:T(8,128)(2,1)S(1)} %select_bitcast_fusion.2), channel_id=1, source_target_pairs={{0,16},{8,24},{16,0},{24,8},{1,17},{9,25},{17,1},{25,9},{2,18},{10... | collective-permute-start | bytes 1572872 | tf_op jit(solution)/shard_map/ppermute | solution.py:179
  132.5 11.3 %copy-start.10 = (bf16[1024,2048]{1,0:T(8,128)(2,1)S(1)}, bf16[1024,2048]{1,0:T(8,128)(2,1)}, u32[]{:S(2)}) copy-start(bf16[1024,2048]{1,0:T(8,128)(2,1)} %copy-done.9) | copy-start | bytes 12582916
  143.8 14.9 %collective-permute-start.18 = (bf16[4,32,2048]{2,1,0:T(8,128)(2,1)S(1)}, bf16[4,32,2048]{2,1,0:T(8,128)(2,1)S(1)}, u32[]{:S(2)}, u32[]{:S(2)}) collective-permute-start(bf16[4,32,2048]{2,1,0:T(8,128)(2,1)S(1)} %fusion.51), channel_id=1, source_target_pairs={{0,1},{1,0},{2,3},{3,2},{4,5},{5,4},{6,7},{7,6},{8,9},{9,8},{10,11... | collective-permute-start | bytes 1572872 | tf_op jit(solution)/shard_map/ppermute | solution.py:179
  145.3 2.2 %copy-start.19 = (f32[16,16]{1,0:T(8,128)S(1)}, f32[16,16]{1,0:T(8,128)}, u32[]{:S(2)}) copy-start(f32[16,16]{1,0:T(8,128)} %get-tuple-element.44) | copy-start | bytes 3076
  145.4 34.4 %collective-permute-start.22 = (bf16[8,32,2048]{2,1,0:T(8,128)(2,1)S(1)}, bf16[8,32,2048]{2,1,0:T(8,128)(2,1)S(1)}, u32[]{:S(2)}, u32[]{:S(2)}) collective-permute-start(bf16[8,32,2048]{2,1,0:T(8,128)(2,1)S(1)} %fusion.30), channel_id=1, source_target_pairs={{0,1},{1,0},{2,3},{3,2},{4,5},{5,4},{6,7},{7,6},{8,9},{9,8},{10,11... | collective-permute-start | bytes 3145736 | tf_op jit(solution)/shard_map/ppermute | solution.py:179
  159.0 21.6 %collective-permute-start.19 = (bf16[1,64,2048]{2,1,0:T(8,128)(2,1)S(1)}, bf16[1,64,2048]{2,1,0:T(8,128)(2,1)S(1)}, u32[]{:S(2)}, u32[]{:S(2)}) collective-permute-start(bf16[1,64,2048]{2,1,0:T(8,128)(2,1)S(1)} %select_bitcast_fusion.5), channel_id=1, source_target_pairs={{0,4},{1,5},{2,6},{3,7},{4,0},{5,1},{6,2},{7,3},{8,12},{9,13},{10,... | collective-permute-start | bytes 786440 | tf_op jit(solution)/shard_map/ppermute | solution.py:179
  180.5 22.7 %collective-permute-start.23 = (bf16[2,64,2048]{2,1,0:T(8,128)(2,1)S(1)}, bf16[2,64,2048]{2,1,0:T(8,128)(2,1)S(1)}, u32[]{:S(2)}, u32[]{:S(2)}) collective-permute-start(bf16[2,64,2048]{2,1,0:T(8,128)(2,1)S(1)} %fusion.52), channel_id=1, source_target_pairs={{0,4},{1,5},{2,6},{3,7},{4,0},{5,1},{6,2},{7,3},{8,12},{9,13},{10,... | collective-permute-start | bytes 1572872 | tf_op jit(solution)/shard_map/ppermute | solution.py:179
  180.7 23.6 %collective-permute-start.20 = (bf16[1,32,2048]{2,1,0:T(8,128)(2,1)S(1)}, bf16[1,32,2048]{2,1,0:T(8,128)(2,1)S(1)}, u32[]{:S(2)}, u32[]{:S(2)}) collective-permute-start(bf16[1,32,2048]{2,1,0:T(8,128)(2,1)S(1)} %select_bitcast_fusion.7), channel_id=1, source_target_pairs={{0,2},{1,3},{2,0},{3,1},{4,6},{5,7},{6,4},{7,5},{8,10},{9,11},{10,... | collective-permute-start | bytes 393224 | tf_op jit(solution)/shard_map/ppermute | solution.py:179
  203.4 14.3 %copy-start.1 = (bf16[1024,1024]{1,0:T(8,128)(2,1)S(1)}, bf16[1024,1024]{1,0:T(8,128)(2,1)}, u32[]{:S(2)}) copy-start(bf16[1024,1024]{1,0:T(8,128)(2,1)} %param.8) | copy-start | bytes 6291460
  203.5 8.3 %collective-permute-start.24 = (bf16[1,64,2048]{2,1,0:T(8,128)(2,1)S(1)}, bf16[1,64,2048]{2,1,0:T(8,128)(2,1)S(1)}, u32[]{:S(2)}, u32[]{:S(2)}) collective-permute-start(bf16[1,64,2048]{2,1,0:T(8,128)(2,1)S(1)} %select_bitcast_fusion.4), channel_id=1, source_target_pairs={{0,16},{8,24},{16,0},{24,8},{1,17},{9,25},{17,1},{25,9},{2,18},{10... | collective-permute-start | bytes 786440 | tf_op jit(solution)/shard_map/ppermute | solution.py:179
  211.9 5.0 %collective-permute-start.25 = (bf16[1,32,2048]{2,1,0:T(8,128)(2,1)S(1)}, bf16[1,32,2048]{2,1,0:T(8,128)(2,1)S(1)}, u32[]{:S(2)}, u32[]{:S(2)}) collective-permute-start(bf16[1,32,2048]{2,1,0:T(8,128)(2,1)S(1)} %select_bitcast_fusion.6), channel_id=1, source_target_pairs={{0,2},{1,3},{2,0},{3,1},{4,6},{5,7},{6,4},{7,5},{8,10},{9,11},{10,... | collective-permute-start | bytes 393224 | tf_op jit(solution)/shard_map/ppermute | solution.py:179

commit v3 on v2

--- a/solution.py
+++ b/solution.py
@@ -243,7 +243,11 @@
     query_term = dot(normed, grad_query, TN).astype(jnp.bfloat16)
     query_part, left_over = halved(query_term, places, low_first[:split])
     keyval_term = dot(normed_frame, jnp.concatenate([grad_key, grad_value], axis=1), TN)
-    keyval_share, none = halved(keyval_term.astype(jnp.bfloat16), places, lon_first)
+    keyval_part, left_keyval = halved(keyval_term.astype(jnp.bfloat16), places, lon_first[:1])
+    keyval_part, grad_key, grad_value = lax.optimization_barrier(
+        (keyval_part, grad_key, grad_value)
+    )
+    keyval_share, none = halved(keyval_part, left_keyval, lon_first[1:])
     pair_part = jnp.concatenate([query_part, out_part], axis=1)
     pair_share, none = halved(pair_part, left_over, low_first[split:])
     qkv_share = jnp.concatenate([pair_share[:, :width], keyval_share], axis=1)

time: 218 us -> 221 us (1.014)
  starting transfers between devices: 39.3 us -> 44.4 us
    ppermute x4, waiting for transfers between devices: 7.94 us -> 34.6 us  [to_next(): lax.ppermute(value, axis, [(i, (i + 1) % count) for i in range(count)])]
    ppermute x12, waiting for transfers between devices: 82.6 us -> 59.3 us  [halved(): came = lax.ppermute(sent, axis, pairs)]
    ppermute x12, starting transfers between devices: 6.8 us -> 11.5 us  [halved(): came = lax.ppermute(sent, axis, pairs)]
    ppermute x2, starting transfers between devices: 6.14 us -> 10.5 us  [across_pole(): return lax.ppermute(value, ('lat', 'lon'), pairs)]
    ppermute x2, waiting for transfers between devices: 4.04 us -> 0.01 us  [across_pole(): return lax.ppermute(value, ('lat', 'lon'), pairs)]
    ppermute x4, starting transfers between devices: 16.9 us -> 13.7 us  [to_previous(): lax.ppermute(value, axis, [((i + 1) % count, i) for i in range(count)])]
  transfers between devices with their start and end apart: 26 -> 26, of which waited for: 14 -> 11; matrix products, arithmetic and copies ran while one was open for 16% -> 16% of each run, Pallas kernels for 0% -> 0%
where the time goes in v3:
time: 221 us; the launch traced here: 220 us
  waiting for transfers between devices  100 us (45%)
  starting transfers between devices  44.4 us (20%)
  other arithmetic  24 us (11%)
  matrix products  23.9 us (11%)
  Pallas kernels  21.2 us (10%)
  local copies, waits for them, and re-layouts  4.79 us (2%)
    ppermute x12, waiting for transfers between devices, halved(): came = lax.ppermute(sent, axis, pairs)  59.3 us
    ppermute x4, waiting for transfers between devices, to_next(): lax.ppermute(value, axis, [(i, (i + 1) % count) for i in range(count)])  34.6 us
    dot_general x10, matrix products, dot(): return lax.dot_general(a, b, dims, preferred_element_type=jnp.float32)  23.9 us
    pallas_call x1, Pallas kernels, attention(): pl.pallas_call(kernel, grid=(pairs,), in_specs=[one(cells), one(frame_cel...  21.2 us
    ppermute x4, starting transfers between devices, to_previous(): lax.ppermute(value, axis, [((i + 1) % count, i) for i in range(count)])  13.7 us
    ppermute x12, starting transfers between devices, halved(): came = lax.ppermute(sent, axis, pairs)  11.5 us
    ppermute x2, starting transfers between devices, across_pole(): return lax.ppermute(value, ('lat', 'lon'), pairs)  10.5 us
    ppermute x4, waiting for transfers between devices, to_previous(): lax.ppermute(value, axis, [((i + 1) % count, i) for i in range(count)])  6.59 us
  transfers between devices with their start and end apart: 26, of which 11 were waited for; matrix products, arithmetic and copies ran while one was open for 16% of the time, Pallas kernels for 0%

profile of v3, /device:TPU:0, one launch (start us, length us, event | category | flops | bytes accessed | tf_op | source)
XLA Modules:
  0.0 220.1 jit_solution(10970080064905228814)
XLA Ops:
  0.7 1.9 fusion.71
  2.6 5.9 %collective-permute-start = (bf16[6,16,1024]{2,1,0:T(8,128)(2,1)S(1)}, bf16[6,16,1024]{2,1,0:T(8,128)(2,1)S(1)}, u32[]{:S(2)}, u32[]{:S(2)}) collective-permute-start(bf16[6,16,1024]{2,1,0:T(8,128)(2,1)S(1)} %rev.6), channel_id=1, source_target_pairs={{0,4},{1,5},{2,6},{3,7},{4,0},{5,1},{6,2},{7,3},{24,28},{25,29},{2... | collective-permute-start | bytes 589832 | tf_op jit(solution)/shard_map/ppermute | solution.py:164
  8.5 2.0 collective-permute-start.1
  10.5 1.3 collective-permute-start.2
  11.8 1.8 fusion.70
  13.6 1.5 collective-permute-start.5
  15.1 3.2 %collective-permute-start.6 = (bf16[16,8,1024]{2,1,0:T(8,128)(2,1)S(1)}, bf16[16,8,1024]{2,1,0:T(8,128)(2,1)}, u32[]{:S(2)}, u32[]{:S(2)}) collective-permute-start(bf16[16,8,1024]{2,1,0:T(8,128)(2,1)S(1)} %get-tuple-element.29), channel_id=1, source_target_pairs={{1,0},{2,1},{3,2},{4,3},{5,4},{6,5},{7,6},{0,7},{9,8},{10,9},{11,1... | collective-permute-start | bytes 786440 | tf_op jit(solution)/shard_map/ppermute | solution.py:143
  18.5 0.6 multiply_multiply_fusion
  19.5 2.5 %fusion.27.refs_0_ = bf16[256,1024]{1,0:T(8,128)(2,1)S(1)} fusion(bf16[256,1024]{1,0:T(8,128)(2,1)S(1)} %fusion.46, bf16[1024,3072]{1,0:T(8,128)(2,1)} %param.7), kind=kOutput, calls=%fused_computation.38 | convolution fusion | flops 537133056 | bytes 3145728 | tf_op jit(solution)/shard_map/dot_general | solution.py:21
  22.0 1.0 broadcast_select_fusion.2
  23.2 0.7 convolution_convert_fusion.3.refs_3_
  23.9 4.8 %collective-permute-start.4 = (bf16[12,8,1024]{2,1,0:T(8,128)(2,1)S(1)}, bf16[12,8,1024]{2,1,0:T(8,128)(2,1)S(1)}, u32[]{:S(2)}, u32[]{:S(2)}) collective-permute-start(bf16[12,8,1024]{2,1,0:T(8,128)(2,1)S(1)} %get-tuple-element.39), channel_id=1, source_target_pairs={{1,0},{2,1},{3,2},{4,3},{5,4},{6,5},{7,6},{0,7},{9,8},{10,9},{11,1... | collective-permute-start | bytes 589832 | tf_op jit(solution)/shard_map/ppermute | solution.py:143
  28.7 7.2 %collective-permute-done.3 = bf16[12,8,1024]{2,1,0:T(8,128)(2,1)S(1)} collective-permute-done((bf16[12,8,1024]{2,1,0:T(8,128)(2,1)S(1)}, bf16[12,8,1024]{2,1,0:T(8,128)(2,1)S(1)}, u32[]{:S(2)}, u32[]{:S(2)}) %collective-permute-start.3) | collective-permute-done | bytes 196640 | tf_op jit(solution)/shard_map/ppermute | solution.py:138
  35.9 2.3 %collective-permute-done.4 = bf16[12,8,1024]{2,1,0:T(8,128)(2,1)S(1)} collective-permute-done((bf16[12,8,1024]{2,1,0:T(8,128)(2,1)S(1)}, bf16[12,8,1024]{2,1,0:T(8,128)(2,1)S(1)}, u32[]{:S(2)}, u32[]{:S(2)}) %collective-permute-start.4) | collective-permute-done | bytes 196640 | tf_op jit(solution)/shard_map/ppermute | solution.py:143
  38.2 3.0 %multiply_reduce_fusion = (f32[28,32]{1,0:T(8,128)S(1)}, f32[28,32,1024]{2,1,0:T(8,128)}) fusion(bf16[6,8,1024]{2,1,0:T(8,128)(2,1)S(1)} %get-tuple-element.47, bf16[6,8,1024]{2,1,0:T(8,128)(2,1)S(1)} %get-tuple-element.45, bf16[6,16,1024]{2,1,0:T(8,128)(2,1)S(1)} %get-tuple-element.49, bf16[16,8,1024]{2,1,0:T(8,128)(2,1)} %collective-permute-done.6, ...), kind=kLoop, calls=%fused_computation.12 | loop fusion | flops 18349184 | bytes 5508608 | tf_op jit(solution)/shard_map/reduce_sum | solution.py:218
  41.3 2.4 %fusion.7 = bf16[896,1024]{1,0:T(8,128)(2,1)S(1)} fusion(f32[28,32,1024]{2,1,0:T(8,128)} %get-tuple-element.21, f32[1024]{0:T(1024)S(1)} %copy-done.13, f32[896]{0:T(1024)S(1)} %rsqrt.29), kind=kLoop, calls=%fused_computation.11 | loop fusion | flops 2752512 | bytes 5512704 | tf_op jit(solution)/shard_map/convert_element_type | solution.py:219
  43.7 6.4 %fusion.8.refs_1_.refs_2_ = bf16[896,2048]{1,0:T(8,128)(2,1)S(1)} fusion(bf16[896,1024]{1,0:T(8,128)(2,1)S(1)} %fusion.7, bf16[1024,3072]{1,0:T(8,128)(2,1)} %param.7), kind=kOutput, calls=%fused_computation.13 | convolution fusion | flops 3759931392 | bytes 9699328 | tf_op jit(solution)/shard_map/dot_general | solution.py:21
  50.2 21.2 %shard_map.84 = (bf16[256,1024]{1,0:T(8,128)(2,1)S(1)}, bf16[256,1024]{1,0:T(8,128)(2,1)S(1)}, bf16[896,1024]{1,0:T(8,128)(2,1)S(1)}, bf16[896,1024]{1,0:T(8,128)(2,1)S(1)}) custom-call(bf16[256,1024]{1,0:T(8,128)(2,1)S(1)} %fusion.27.refs_0_, bf16[896,2048]{1,0:T(8,128)(2,1)S(1)} %fusion.8.refs_1_.refs_2_, bf16[896,2048]{1,0:T(8,128)(2,1)S(1)} %fusion.8.refs_1_.refs_2_, ...), custom_call_target="tpu_custom_call" | custom-call | flops 4026531840 | bytes 16777216 | tf_op jit(solution)/shard_map/pallas_call | solution.py:122
  71.4 0.7 convolution_convert_fusion.2
  72.4 0.8 copy-done.7
  73.2 0.8 convolution_convert_fusion.1
  74.2 5.2 %convolution_convert_fusion = bf16[1024,2048]{1,0:T(8,128)(2,1)S(1)} fusion(bf16[896,1024]{1,0:T(8,128)(2,1)S(1)} %fusion.7, bf16[896,1024]{1,0:T(8,128)(2,1)S(1)} %get-tuple-element.15, bf16[896,1024]{1,0:T(8,128)(2,1)S(1)} %get-tuple-element.14), kind=kOutput, calls=%fused_computation.5 | convolution fusion | flops 3767533568 | bytes 9699328 | tf_op jit(solution)/shard_map/dot_general | solution.py:21
  79.6 0.5 collective-permute-start.7
  80.2 1.7 fusion.20
  81.9 0.6 fusion.33
  82.6 1.8 collective-permute-start.16
  84.4 0.6 fusion.34
  85.1 0.4 collective-permute-start.18
  85.5 1.5 fusion.30
  87.0 10.4 %collective-permute-done.16 = bf16[1,256,1024]{2,1,0:T(8,128)(2,1)S(1)} collective-permute-done((bf16[1,256,1024]{2,1,0:T(8,128)(2,1)S(1)}, bf16[1,256,1024]{2,1,0:T(8,128)(2,1)S(1)}, u32[]{:S(2)}, u32[]{:S(2)}) %collective-permute-start.16) | collective-permute-done | bytes 524320 | tf_op jit(solution)/shard_map/ppermute | solution.py:179
  97.7 10.1 %collective-permute-done.18 = bf16[1,256,1024]{2,1,0:T(8,128)(2,1)S(1)} collective-permute-done((bf16[1,256,1024]{2,1,0:T(8,128)(2,1)S(1)}, bf16[1,256,1024]{2,1,0:T(8,128)(2,1)S(1)}, u32[]{:S(2)}, u32[]{:S(2)}) %collective-permute-start.18) | collective-permute-done | bytes 524320 | tf_op jit(solution)/shard_map/ppermute | solution.py:179
  108.2 0.3 collective-permute-start.19
  108.6 1.3 fusion
  109.8 2.1 fusion.16
  111.9 2.1 fusion.24
  114.1 0.3 convert.19
  114.4 1.1 fusion.68
  115.5 5.8 %collective-permute-done.19 = bf16[4,32,2048]{2,1,0:T(8,128)(2,1)S(1)} collective-permute-done((bf16[4,32,2048]{2,1,0:T(8,128)(2,1)S(1)}, bf16[4,32,2048]{2,1,0:T(8,128)(2,1)S(1)}, u32[]{:S(2)}, u32[]{:S(2)}) %collective-permute-start.19) | collective-permute-done | bytes 524320 | tf_op jit(solution)/shard_map/ppermute | solution.py:179
  121.6 0.7 select_bitcast_fusion.4
  122.6 1.1 fusion.32
  123.7 0.8 collective-permute-start.22
  124.6 1.3 collective-permute-start.10
  125.8 3.5 %collective-permute-start.11 = (bf16[12,8,1024]{2,1,0:T(8,128)(2,1)S(1)}, bf16[12,8,1024]{2,1,0:T(8,128)(2,1)S(1)}, u32[]{:S(2)}, u32[]{:S(2)}) collective-permute-start(bf16[12,8,1024]{2,1,0:T(8,128)(2,1)S(1)} %get-tuple-element.37), channel_id=1, source_target_pairs={{1,0},{2,1},{3,2},{4,3},{5,4},{6,5},{7,6},{0,7},{9,8},{10,9},{11,1... | collective-permute-start | bytes 589832 | tf_op jit(solution)/shard_map/ppermute | solution.py:143
  129.4 27.4 %collective-permute-done.10 = bf16[12,8,1024]{2,1,0:T(8,128)(2,1)S(1)} collective-permute-done((bf16[12,8,1024]{2,1,0:T(8,128)(2,1)S(1)}, bf16[12,8,1024]{2,1,0:T(8,128)(2,1)S(1)}, u32[]{:S(2)}, u32[]{:S(2)}) %collective-permute-start.10) | collective-permute-done | bytes 196640 | tf_op jit(solution)/shard_map/ppermute | solution.py:138
  156.8 4.3 %collective-permute-done.11 = bf16[12,8,1024]{2,1,0:T(8,128)(2,1)S(1)} collective-permute-done((bf16[12,8,1024]{2,1,0:T(8,128)(2,1)S(1)}, bf16[12,8,1024]{2,1,0:T(8,128)(2,1)S(1)}, u32[]{:S(2)}, u32[]{:S(2)}) %collective-permute-start.11) | collective-permute-done | bytes 196640 | tf_op jit(solution)/shard_map/ppermute | solution.py:143
  161.2 0.7 fusion.72
  161.9 0.7 rev.7
  162.6 4.5 %collective-permute-start.12 = (bf16[6,16,1024]{2,1,0:T(8,128)(2,1)}, bf16[6,16,1024]{2,1,0:T(8,128)(2,1)S(1)}, u32[]{:S(2)}, u32[]{:S(2)}) collective-permute-start(bf16[6,16,1024]{2,1,0:T(8,128)(2,1)} %rev.7), channel_id=1, source_target_pairs={{0,4},{1,5},{2,6},{3,7},{4,0},{5,1},{6,2},{7,3},{24,28},{25,29},{2... | collective-permute-start | bytes 589832 | tf_op jit(solution)/shard_map/ppermute | solution.py:164
  167.1 1.3 collective-permute-start.13
  168.5 1.3 collective-permute-start.14
  169.8 1.1 fusion.60
  170.9 1.5 collective-permute-start.21
  172.4 1.6 fusion.13
  174.1 3.1 %collective-permute-done.21 = bf16[1,32,2048]{2,1,0:T(8,128)(2,1)S(1)} collective-permute-done((bf16[1,32,2048]{2,1,0:T(8,128)(2,1)S(1)}, bf16[1,32,2048]{2,1,0:T(8,128)(2,1)S(1)}, u32[]{:S(2)}, u32[]{:S(2)}) %collective-permute-start.21) | collective-permute-done | bytes 131104 | tf_op jit(solution)/shard_map/ppermute | solution.py:179
  177.1 0.6 collective-permute-start.23
  177.8 0.7 slice_multiply_fusion
  178.5 2.2 %collective-permute-start.9 = (bf16[16,8,1024]{2,1,0:T(8,128)(2,1)S(1)}, bf16[16,8,1024]{2,1,0:T(8,128)(2,1)S(1)}, u32[]{:S(2)}, u32[]{:S(2)}) collective-permute-start(bf16[16,8,1024]{2,1,0:T(8,128)(2,1)S(1)} %copy-done.12), channel_id=1, source_target_pairs={{1,0},{2,1},{3,2},{4,3},{5,4},{6,5},{7,6},{0,7},{9,8},{10,9},{11,1... | collective-permute-start | bytes 786440 | tf_op jit(solution)/shard_map/ppermute | solution.py:143
  180.8 23.3 %collective-permute-done.23 = bf16[2,64,2048]{2,1,0:T(8,128)(2,1)S(1)} collective-permute-done((bf16[2,64,2048]{2,1,0:T(8,128)(2,1)S(1)}, bf16[2,64,2048]{2,1,0:T(8,128)(2,1)S(1)}, u32[]{:S(2)}, u32[]{:S(2)}) %collective-permute-start.23) | collective-permute-done | bytes 524320 | tf_op jit(solution)/shard_map/ppermute | solution.py:179
  204.5 1.8 fusion.51
  206.3 4.8 %collective-permute-done.24 = bf16[1,64,2048]{2,1,0:T(8,128)(2,1)S(1)} collective-permute-done((bf16[1,64,2048]{2,1,0:T(8,128)(2,1)S(1)}, bf16[1,64,2048]{2,1,0:T(8,128)(2,1)S(1)}, u32[]{:S(2)}, u32[]{:S(2)}) %collective-permute-start.24) | collective-permute-done | bytes 262176 | tf_op jit(solution)/shard_map/ppermute | solution.py:179
  211.2 5.1 %collective-permute-start.25 = (bf16[1,32,2048]{2,1,0:T(8,128)(2,1)S(1)}, bf16[1,32,2048]{2,1,0:T(8,128)(2,1)S(1)}, u32[]{:S(2)}, u32[]{:S(2)}) collective-permute-start(bf16[1,32,2048]{2,1,0:T(8,128)(2,1)S(1)} %select_bitcast_fusion.5), channel_id=1, source_target_pairs={{0,2},{1,3},{2,0},{3,1},{4,6},{5,7},{6,4},{7,5},{8,10},{9,11},{10,... | collective-permute-start | bytes 393224 | tf_op jit(solution)/shard_map/ppermute | solution.py:179
  216.4 1.1 fusion.50
  217.5 1.8 collective-permute-done.25
  219.3 0.8 maximum_multiply_fusion
  (87 shorter events, 3.7 us)
Async XLA Ops:
  0.6 22.5 %copy-start = (bf16[1024,1024]{1,0:T(8,128)(2,1)S(1)}, bf16[1024,1024]{1,0:T(8,128)(2,1)}, u32[]{:S(2)}) copy-start(bf16[1024,1024]{1,0:T(8,128)(2,1)} %param.8) | copy-start | bytes 6291460
  0.6 17.6 %copy-start.2 = (bf16[16,16,1024]{2,1,0:T(8,128)(2,1)S(1)}, bf16[16,16,1024]{2,1,0:T(8,128)(2,1)}, u32[]{:S(2)}) copy-start(bf16[16,16,1024]{2,1,0:T(8,128)(2,1)} %param.5) | copy-start | bytes 1572868
  0.7 18.6 %copy-start.13 = (f32[1024]{0:T(1024)S(1)}, f32[1024]{0:T(1024)}, u32[]{:S(2)}) copy-start(f32[1024]{0:T(1024)} %param.6) | copy-start | bytes 12292
  2.6 19.4 %collective-permute-start = (bf16[6,16,1024]{2,1,0:T(8,128)(2,1)S(1)}, bf16[6,16,1024]{2,1,0:T(8,128)(2,1)S(1)}, u32[]{:S(2)}, u32[]{:S(2)}) collective-permute-start(bf16[6,16,1024]{2,1,0:T(8,128)(2,1)S(1)} %rev.6), channel_id=1, source_target_pairs={{0,4},{1,5},{2,6},{3,7},{4,0},{5,1},{6,2},{7,3},{24,28},{25,29},{2... | collective-permute-start | bytes 589832 | tf_op jit(solution)/shard_map/ppermute | solution.py:164
  8.5 13.5 %collective-permute-start.1 = (bf16[6,16,1024]{2,1,0:T(8,128)(2,1)}, bf16[6,16,1024]{2,1,0:T(8,128)(2,1)}, u32[]{:S(2)}, u32[]{:S(2)}) collective-permute-start(bf16[6,16,1024]{2,1,0:T(8,128)(2,1)} %get-tuple-element.30), channel_id=1, source_target_pairs={{0,8},{8,16},{16,24},{1,9},{9,17},{17,25},{2,10},{10,18},{18,26},{... | collective-permute-start | bytes 589832 | tf_op jit(solution)/shard_map/ppermute | solution.py:153
  10.5 11.5 %collective-permute-start.2 = (bf16[6,16,1024]{2,1,0:T(8,128)(2,1)S(1)}, bf16[6,16,1024]{2,1,0:T(8,128)(2,1)}, u32[]{:S(2)}, u32[]{:S(2)}) collective-permute-start(bf16[6,16,1024]{2,1,0:T(8,128)(2,1)S(1)} %get-tuple-element.32), channel_id=1, source_target_pairs={{8,0},{16,8},{24,16},{9,1},{17,9},{25,17},{10,2},{18,10},{26,18},{... | collective-permute-start | bytes 589832 | tf_op jit(solution)/shard_map/ppermute | solution.py:148
  13.6 24.6 %collective-permute-start.5 = (bf16[16,8,1024]{2,1,0:T(8,128)(2,1)}, bf16[16,8,1024]{2,1,0:T(8,128)(2,1)}, u32[]{:S(2)}, u32[]{:S(2)}) collective-permute-start(bf16[16,8,1024]{2,1,0:T(8,128)(2,1)} %get-tuple-element.28), channel_id=1, source_target_pairs={{0,1},{1,2},{2,3},{3,4},{4,5},{5,6},{6,7},{7,0},{8,9},{9,10},{10,1... | collective-permute-start | bytes 786440 | tf_op jit(solution)/shard_map/ppermute | solution.py:138
  15.1 23.1 %collective-permute-start.6 = (bf16[16,8,1024]{2,1,0:T(8,128)(2,1)S(1)}, bf16[16,8,1024]{2,1,0:T(8,128)(2,1)}, u32[]{:S(2)}, u32[]{:S(2)}) collective-permute-start(bf16[16,8,1024]{2,1,0:T(8,128)(2,1)S(1)} %get-tuple-element.29), channel_id=1, source_target_pairs={{1,0},{2,1},{3,2},{4,3},{5,4},{6,5},{7,6},{0,7},{9,8},{10,9},{11,1... | collective-permute-start | bytes 786440 | tf_op jit(solution)/shard_map/ppermute | solution.py:143
  19.4 2.6 %copy-start.9 = (bf16[256,1024]{1,0:T(8,128)(2,1)}, bf16[256,1024]{1,0:T(8,128)(2,1)S(1)}, u32[]{:S(2)}) copy-start(bf16[256,1024]{1,0:T(8,128)(2,1)S(1)} %fusion.46) | copy-start | bytes 1572868
  19.4 3.7 %copy-start.6 = (bf16[16,16,1024]{2,1,0:T(8,128)(2,1)S(1)}, bf16[16,16,1024]{2,1,0:T(8,128)(2,1)}, u32[]{:S(2)}) copy-start(bf16[16,16,1024]{2,1,0:T(8,128)(2,1)} %param.9) | copy-start | bytes 1572868
  23.1 12.8 %collective-permute-start.3 = (bf16[12,8,1024]{2,1,0:T(8,128)(2,1)S(1)}, bf16[12,8,1024]{2,1,0:T(8,128)(2,1)S(1)}, u32[]{:S(2)}, u32[]{:S(2)}) collective-permute-start(bf16[12,8,1024]{2,1,0:T(8,128)(2,1)S(1)} %get-tuple-element.38), channel_id=1, source_target_pairs={{0,1},{1,2},{2,3},{3,4},{4,5},{5,6},{6,7},{7,0},{8,9},{9,10},{10,1... | collective-permute-start | bytes 589832 | tf_op jit(solution)/shard_map/ppermute | solution.py:138
  23.1 15.1 %copy-start.3 = (bf16[16,16,1024]{2,1,0:T(8,128)(2,1)S(1)}, bf16[16,16,1024]{2,1,0:T(8,128)(2,1)}, u32[]{:S(2)}) copy-start(bf16[16,16,1024]{2,1,0:T(8,128)(2,1)} %param.5) | copy-start | bytes 1572868
  23.9 14.3 %collective-permute-start.4 = (bf16[12,8,1024]{2,1,0:T(8,128)(2,1)S(1)}, bf16[12,8,1024]{2,1,0:T(8,128)(2,1)S(1)}, u32[]{:S(2)}, u32[]{:S(2)}) collective-permute-start(bf16[12,8,1024]{2,1,0:T(8,128)(2,1)S(1)} %get-tuple-element.39), channel_id=1, source_target_pairs={{1,0},{2,1},{3,2},{4,3},{5,4},{6,5},{7,6},{0,7},{9,8},{10,9},{11,1... | collective-permute-start | bytes 589832 | tf_op jit(solution)/shard_map/ppermute | solution.py:143
  50.2 21.2 %copy-start.10 = (bf16[256,1024]{1,0:T(8,128)(2,1)S(1)}, bf16[256,1024]{1,0:T(8,128)(2,1)}, u32[]{:S(2)}) copy-start(bf16[256,1024]{1,0:T(8,128)(2,1)} %copy-done.9) | copy-start | bytes 1572868
  72.1 1.0 copy-start.7
  72.3 9.6 %collective-permute-start.15 = (bf16[2,256,1024]{2,1,0:T(8,128)(2,1)S(1)}, bf16[2,256,1024]{2,1,0:T(8,128)(2,1)S(1)}, u32[]{:S(2)}, u32[]{:S(2)}) collective-permute-start(bf16[2,256,1024]{2,1,0:T(8,128)(2,1)S(1)} %fusion.31), channel_id=1, source_target_pairs={{0,8},{8,0},{16,24},{24,16},{1,9},{9,1},{17,25},{25,17},{2,10},{10... | collective-permute-start | bytes 3145736 | tf_op jit(solution)/shard_map/ppermute | solution.py:179
  74.0 6.2 %slice-start = ((s8[6291456]{0:T(1024)(128)(4,1)}), s8[4194304]{0:T(1024)(128)(4,1)S(1)}, s32[]{:S(2)}) async-start(s8[6291456]{0:T(1024)(128)(4,1)} %bitcast.231), calls=%async_computation | async-start | bytes 8388608
  74.1 10.3 %collective-permute-start.17 = (bf16[2,256,1024]{2,1,0:T(8,128)(2,1)S(1)}, bf16[2,256,1024]{2,1,0:T(8,128)(2,1)S(1)}, u32[]{:S(2)}, u32[]{:S(2)}) collective-permute-start(bf16[2,256,1024]{2,1,0:T(8,128)(2,1)S(1)} %select_bitcast_fusion), channel_id=1, source_target_pairs={{0,8},{8,0},{16,24},{24,16},{1,9},{9,1},{17,25},{25,17},{2,10},{10... | collective-permute-start | bytes 3145736 | tf_op jit(solution)/shard_map/ppermute | solution.py:179
  74.2 6.0 %slice-start.1 = ((s8[6291456]{0:T(1024)(128)(4,1)}), s8[2097152]{0:T(1024)(128)(4,1)S(1)}, s32[]{:S(2)}) async-start(s8[6291456]{0:T(1024)(128)(4,1)} %bitcast.231), calls=%async_computation.1 | async-start | bytes 4194304
  79.6 28.9 %collective-permute-start.7 = (bf16[2,256,2048]{2,1,0:T(8,128)(2,1)S(1)}, bf16[2,256,2048]{2,1,0:T(8,128)(2,1)S(1)}, u32[]{:S(2)}, u32[]{:S(2)}) collective-permute-start(bf16[2,256,2048]{2,1,0:T(8,128)(2,1)S(1)} %fusion.11), channel_id=1, source_target_pairs={{0,8},{8,0},{16,24},{24,16},{1,9},{9,1},{17,25},{25,17},{2,10},{10... | collective-permute-start | bytes 6291464 | tf_op jit(solution)/shard_map/ppermute | solution.py:179
  82.6 2.9 %copy-start.4 = (bf16[16,16,1024]{2,1,0:T(8,128)(2,1)S(1)}, bf16[16,16,1024]{2,1,0:T(8,128)(2,1)}, u32[]{:S(2)}) copy-start(bf16[16,16,1024]{2,1,0:T(8,128)(2,1)} %param.5) | copy-start | bytes 1572868
  82.6 14.8 %collective-permute-start.16 = (bf16[1,256,1024]{2,1,0:T(8,128)(2,1)S(1)}, bf16[1,256,1024]{2,1,0:T(8,128)(2,1)S(1)}, u32[]{:S(2)}, u32[]{:S(2)}) collective-permute-start(bf16[1,256,1024]{2,1,0:T(8,128)(2,1)S(1)} %select_bitcast_fusion.2), channel_id=1, source_target_pairs={{0,16},{8,24},{16,0},{24,8},{1,17},{9,25},{17,1},{25,9},{2,18},{10... | collective-permute-start | bytes 1572872 | tf_op jit(solution)/shard_map/ppermute | solution.py:179
  85.1 22.7 %collective-permute-start.18 = (bf16[1,256,1024]{2,1,0:T(8,128)(2,1)S(1)}, bf16[1,256,1024]{2,1,0:T(8,128)(2,1)S(1)}, u32[]{:S(2)}, u32[]{:S(2)}) collective-permute-start(bf16[1,256,1024]{2,1,0:T(8,128)(2,1)S(1)} %select_bitcast_fusion.1), channel_id=1, source_target_pairs={{0,16},{8,24},{16,0},{24,8},{1,17},{9,25},{17,1},{25,9},{2,18},{10... | collective-permute-start | bytes 1572872 | tf_op jit(solution)/shard_map/ppermute | solution.py:179
  108.2 13.1 %collective-permute-start.19 = (bf16[4,32,2048]{2,1,0:T(8,128)(2,1)S(1)}, bf16[4,32,2048]{2,1,0:T(8,128)(2,1)S(1)}, u32[]{:S(2)}, u32[]{:S(2)}) collective-permute-start(bf16[4,32,2048]{2,1,0:T(8,128)(2,1)S(1)} %fusion.53), channel_id=1, source_target_pairs={{0,1},{1,0},{2,3},{3,2},{4,5},{5,4},{6,7},{7,6},{8,9},{9,8},{10,11... | collective-permute-start | bytes 1572872 | tf_op jit(solution)/shard_map/ppermute | solution.py:179
  114.1 15.3 %copy-start.5 = (f32[896,1024]{1,0:T(8,128)}, f32[896,1024]{1,0:T(8,128)S(1)}, u32[]{:S(2)}) copy-start(f32[896,1024]{1,0:T(8,128)S(1)} %fusion.24) | copy-start | bytes 11010052
  122.3 46.1 %collective-permute-start.20 = (bf16[1,64,2048]{2,1,0:T(8,128)(2,1)}, bf16[1,64,2048]{2,1,0:T(8,128)(2,1)}, u32[]{:S(2)}, u32[]{:S(2)}) collective-permute-start(bf16[1,64,2048]{2,1,0:T(8,128)(2,1)} %select_bitcast_fusion.4), channel_id=1, source_target_pairs={{0,4},{1,5},{2,6},{3,7},{4,0},{5,1},{6,2},{7,3},{8,12},{9,13},{10,... | collective-permute-start | bytes 786440 | tf_op jit(solution)/shard_map/ppermute | solution.py:179
  123.7 47.1 %collective-permute-start.22 = (bf16[8,32,2048]{2,1,0:T(8,128)(2,1)}, bf16[8,32,2048]{2,1,0:T(8,128)(2,1)}, u32[]{:S(2)}, u32[]{:S(2)}) collective-permute-start(bf16[8,32,2048]{2,1,0:T(8,128)(2,1)} %fusion.32), channel_id=1, source_target_pairs={{0,1},{1,0},{2,3},{3,2},{4,5},{5,4},{6,7},{7,6},{8,9},{9,8},{10,11... | collective-permute-start | bytes 3145736 | tf_op jit(solution)/shard_map/ppermute | solution.py:179
  124.6 32.2 %collective-permute-start.10 = (bf16[12,8,1024]{2,1,0:T(8,128)(2,1)S(1)}, bf16[12,8,1024]{2,1,0:T(8,128)(2,1)S(1)}, u32[]{:S(2)}, u32[]{:S(2)}) collective-permute-start(bf16[12,8,1024]{2,1,0:T(8,128)(2,1)S(1)} %get-tuple-element.36), channel_id=1, source_target_pairs={{0,1},{1,2},{2,3},{3,4},{4,5},{5,6},{6,7},{7,0},{8,9},{9,10},{10,1... | collective-permute-start | bytes 589832 | tf_op jit(solution)/shard_map/ppermute | solution.py:138
  125.8 35.2 %collective-permute-start.11 = (bf16[12,8,1024]{2,1,0:T(8,128)(2,1)S(1)}, bf16[12,8,1024]{2,1,0:T(8,128)(2,1)S(1)}, u32[]{:S(2)}, u32[]{:S(2)}) collective-permute-start(bf16[12,8,1024]{2,1,0:T(8,128)(2,1)S(1)} %get-tuple-element.37), channel_id=1, source_target_pairs={{1,0},{2,1},{3,2},{4,3},{5,4},{6,5},{7,6},{0,7},{9,8},{10,9},{11,1... | collective-permute-start | bytes 589832 | tf_op jit(solution)/shard_map/ppermute | solution.py:143
  129.3 75.1 %collective-permute-start.8 = (bf16[16,8,1024]{2,1,0:T(8,128)(2,1)}, bf16[16,8,1024]{2,1,0:T(8,128)(2,1)}, u32[]{:S(2)}, u32[]{:S(2)}) collective-permute-start(bf16[16,8,1024]{2,1,0:T(8,128)(2,1)} %get-tuple-element.24), channel_id=1, source_target_pairs={{0,1},{1,2},{2,3},{3,4},{4,5},{5,6},{6,7},{7,0},{8,9},{9,10},{10,1... | collective-permute-start | bytes 786440 | tf_op jit(solution)/shard_map/ppermute | solution.py:138
  162.6 15.9 %collective-permute-start.12 = (bf16[6,16,1024]{2,1,0:T(8,128)(2,1)}, bf16[6,16,1024]{2,1,0:T(8,128)(2,1)S(1)}, u32[]{:S(2)}, u32[]{:S(2)}) collective-permute-start(bf16[6,16,1024]{2,1,0:T(8,128)(2,1)} %rev.7), channel_id=1, source_target_pairs={{0,4},{1,5},{2,6},{3,7},{4,0},{5,1},{6,2},{7,3},{24,28},{25,29},{2... | collective-permute-start | bytes 589832 | tf_op jit(solution)/shard_map/ppermute | solution.py:164
  167.1 13.6 %collective-permute-start.13 = (bf16[6,16,1024]{2,1,0:T(8,128)(2,1)}, bf16[6,16,1024]{2,1,0:T(8,128)(2,1)S(1)}, u32[]{:S(2)}, u32[]{:S(2)}) collective-permute-start(bf16[6,16,1024]{2,1,0:T(8,128)(2,1)} %get-tuple-element.33), channel_id=1, source_target_pairs={{0,8},{8,16},{16,24},{1,9},{9,17},{17,25},{2,10},{10,18},{18,26},{... | collective-permute-start | bytes 589832 | tf_op jit(solution)/shard_map/ppermute | solution.py:153
  168.5 12.3 %collective-permute-start.14 = (bf16[6,16,1024]{2,1,0:T(8,128)(2,1)S(1)}, bf16[6,16,1024]{2,1,0:T(8,128)(2,1)S(1)}, u32[]{:S(2)}, u32[]{:S(2)}) collective-permute-start(bf16[6,16,1024]{2,1,0:T(8,128)(2,1)S(1)} %get-tuple-element.35), channel_id=1, source_target_pairs={{8,0},{16,8},{24,16},{9,1},{17,9},{25,17},{10,2},{18,10},{26,18},{... | collective-permute-start | bytes 589832 | tf_op jit(solution)/shard_map/ppermute | solution.py:148
  170.9 6.3 %collective-permute-start.21 = (bf16[1,32,2048]{2,1,0:T(8,128)(2,1)S(1)}, bf16[1,32,2048]{2,1,0:T(8,128)(2,1)S(1)}, u32[]{:S(2)}, u32[]{:S(2)}) collective-permute-start(bf16[1,32,2048]{2,1,0:T(8,128)(2,1)S(1)} %select_bitcast_fusion.6), channel_id=1, source_target_pairs={{0,2},{1,3},{2,0},{3,1},{4,6},{5,7},{6,4},{7,5},{8,10},{9,11},{10,... | collective-permute-start | bytes 393224 | tf_op jit(solution)/shard_map/ppermute | solution.py:179
  174.0 4.5 %copy-start.12 = (bf16[16,8,1024]{2,1,0:T(8,128)(2,1)S(1)}, bf16[16,8,1024]{2,1,0:T(8,128)(2,1)}, u32[]{:S(2)}) copy-start(bf16[16,8,1024]{2,1,0:T(8,128)(2,1)} %get-tuple-element.25) | copy-start | bytes 786436
  177.1 26.9 %collective-permute-start.23 = (bf16[2,64,2048]{2,1,0:T(8,128)(2,1)S(1)}, bf16[2,64,2048]{2,1,0:T(8,128)(2,1)S(1)}, u32[]{:S(2)}, u32[]{:S(2)}) collective-permute-start(bf16[2,64,2048]{2,1,0:T(8,128)(2,1)S(1)} %fusion.54), channel_id=1, source_target_pairs={{0,4},{1,5},{2,6},{3,7},{4,0},{5,1},{6,2},{7,3},{8,12},{9,13},{10,... | collective-permute-start | bytes 1572872 | tf_op jit(solution)/shard_map/ppermute | solution.py:179
  178.5 26.0 %copy-start.11 = (f32[256,1024]{1,0:T(8,128)S(1)}, f32[256,1024]{1,0:T(8,128)}, u32[]{:S(2)}) copy-start(f32[256,1024]{1,0:T(8,128)} %fusion.20) | copy-start | bytes 3145732
  178.5 26.0 %collective-permute-start.9 = (bf16[16,8,1024]{2,1,0:T(8,128)(2,1)S(1)}, bf16[16,8,1024]{2,1,0:T(8,128)(2,1)S(1)}, u32[]{:S(2)}, u32[]{:S(2)}) collective-permute-start(bf16[16,8,1024]{2,1,0:T(8,128)(2,1)S(1)} %copy-done.12), channel_id=1, source_target_pairs={{1,0},{2,1},{3,2},{4,3},{5,4},{6,5},{7,6},{0,7},{9,8},{10,9},{11,1... | collective-permute-start | bytes 786440 | tf_op jit(solution)/shard_map/ppermute | solution.py:143
  204.3 6.7 %collective-permute-start.24 = (bf16[1,64,2048]{2,1,0:T(8,128)(2,1)S(1)}, bf16[1,64,2048]{2,1,0:T(8,128)(2,1)S(1)}, u32[]{:S(2)}, u32[]{:S(2)}) collective-permute-start(bf16[1,64,2048]{2,1,0:T(8,128)(2,1)S(1)} %select_bitcast_fusion.3), channel_id=1, source_target_pairs={{0,16},{8,24},{16,0},{24,8},{1,17},{9,25},{17,1},{25,9},{2,18},{10... | collective-permute-start | bytes 786440 | tf_op jit(solution)/shard_map/ppermute | solution.py:179
  204.5 11.9 %copy-start.8 = (bf16[16,16,1024]{2,1,0:T(8,128)(2,1)S(1)}, bf16[16,16,1024]{2,1,0:T(8,128)(2,1)}, u32[]{:S(2)}) copy-start(bf16[16,16,1024]{2,1,0:T(8,128)(2,1)} %param.9) | copy-start | bytes 1572868
  204.5 11.9 %copy-start.14 = (f32[16,16]{1,0:T(8,128)S(1)}, f32[16,16]{1,0:T(8,128)}, u32[]{:S(2)}) copy-start(f32[16,16]{1,0:T(8,128)} %get-tuple-element.50) | copy-start | bytes 3076
  211.2 9.0 %copy-start.1 = (bf16[1024,1024]{1,0:T(8,128)(2,1)S(1)}, bf16[1024,1024]{1,0:T(8,128)(2,1)}, u32[]{:S(2)}) copy-start(bf16[1024,1024]{1,0:T(8,128)(2,1)} %param.8) | copy-start | bytes 6291460
  211.2 8.1 %collective-permute-start.25 = (bf16[1,32,2048]{2,1,0:T(8,128)(2,1)S(1)}, bf16[1,32,2048]{2,1,0:T(8,128)(2,1)S(1)}, u32[]{:S(2)}, u32[]{:S(2)}) collective-permute-start(bf16[1,32,2048]{2,1,0:T(8,128)(2,1)S(1)} %select_bitcast_fusion.5), channel_id=1, source_target_pairs={{0,2},{1,3},{2,0},{3,1},{4,6},{5,7},{6,4},{7,5},{8,10},{9,11},{10,... | collective-permute-start | bytes 393224 | tf_op jit(solution)/shard_map/ppermute | solution.py:179
